TPU v7x, 256 devices: a whole 4x4x8 slice. The times are simulated.
256 devices in a mesh: row: 32 (over z, y_lo, core), col: 8 (over y_hi, x).
Axes of the slice: x: 4, y: 4 (y_hi: 2, y_lo: 2; y = y_hi * 2 + y_lo), z: 8, core: 2. Of those that a mesh axis runs over, the one named last changes fastest.
Arguments:
- features: bfloat16 [32768, 128], P(('col', 'row')), may hold values from -96 to 96
- weight: bfloat16 [128, 256], replicated, may hold values from -0.5 to 0.5
- bias: float32 [256], replicated, may hold values from -3 to 3
- cotangent: bfloat16 [32768, 256], P(('row', 'col')), may hold values from -6 to 6
- tile_values: bfloat16 [32, 8, 256, 128, 128], P('row', 'col'), may hold values from 0 to 4, as said below
- tile_pos: int32 [32, 8, 2, 256], P('row', 'col'), may hold values from 0 to 31, as said below
- tile_count: int32 [32, 8], P('row', 'col'), may hold values from 0 to 256, as said below
- block_perm: int32 [256], replicated, may hold values from 0 to 255, as said below
Outputs:
- hidden: bfloat16 [32768, 256], P(('row', 'col'))
- weight_grad: float32 [128, 256], replicated
- bias_grad: float32 [256], replicated
Inputs may be any that keep to these rules, and one draw needn't show every extreme that they name: `tile_values`: entries are 0 or a weight of at least 0.25; slots t at or beyond tile_count[r, c] belong to no tile. `tile_pos`: entry [r, c, 0, t] is the slot's tile row, below 8, within row block r, and [r, c, 1, t] its tile column, below 32, within column block c, both in the reordered numbering; the slots of one cell hold distinct positions. `tile_count`: every draw has a cell with 256 live slots. `block_perm`: each aligned run of 8 entries is a permutation of that run's own indices.
All inputs are finite; a program needn't handle non-finite values.
Results may differ from a plain program's by a relative error of at most 0.0059.
Values may be sent and summed in bfloat16 or wider, within the bound.
No kernel may reach another device: no remote copies, remote signals or barrier semaphores. Data moves between devices by JAX's collectives and lax.ppermute only.
A program may use at most 64 MiB of HBM per device.

v0:
```python
import jax
import jax.numpy as jnp
from jax import lax
from jax.sharding import PartitionSpec as P


def local_index(block_perm, tile_axis, block_index, run_length):
    return jnp.take(block_perm, block_index * run_length + tile_axis) - block_index * run_length


def body(features, weight, bias, cotangent, tile_values, tile_pos, tile_count, block_perm):
    row_count = lax.axis_size("row")
    col_count = lax.axis_size("col")
    row_index = lax.axis_index("row")
    col_index = lax.axis_index("col")
    packed = tile_values[0, 0]
    positions = tile_pos[0, 0]
    live_count = tile_count[0, 0]
    max_tiles = packed.shape[0]
    tile_size = packed.shape[1]
    feat_width = features.shape[1]
    row_tiles = block_perm.shape[0] // row_count
    col_tiles = row_tiles * row_count // col_count
    block_tiles = min(64, max_tiles)
    lane_index = jnp.arange(block_tiles, dtype=jnp.int32)
    own_rows = local_index(block_perm, positions[0], row_index, row_tiles)
    own_cols = local_index(block_perm, positions[1], col_index, col_tiles)

    def degree_step(block_step, totals):
        row_acc, col_acc = totals
        slot_number = block_step * block_tiles + lane_index
        is_live = slot_number < live_count
        clamped = jnp.minimum(slot_number, max_tiles - 1)
        values = jnp.take(packed, clamped, axis=0).astype(jnp.float32)
        row_part = jnp.sum(values, axis=2)
        col_part = jnp.sum(values, axis=1)
        row_part = jnp.where(is_live[:, None], row_part, 0.0)
        col_part = jnp.where(is_live[:, None], col_part, 0.0)
        row_acc = row_acc.at[jnp.take(own_rows, clamped)].add(row_part)
        col_acc = col_acc.at[jnp.take(own_cols, clamped)].add(col_part)
        return (row_acc, col_acc)

    degree_blocks = (live_count + block_tiles - 1) // block_tiles
    row_acc, col_acc = lax.fori_loop(
        jnp.int32(0),
        degree_blocks,
        degree_step,
        (
            jnp.zeros((row_tiles, tile_size), jnp.float32),
            jnp.zeros((col_tiles, tile_size), jnp.float32),
        ),
    )
    col_part_flat = col_acc.reshape(col_tiles * tile_size)
    col_share = lax.psum_scatter(col_part_flat, "row", scatter_dimension=0, tiled=True)
    scaled = (lax.rsqrt(1.0 + col_share)[:, None] * features.astype(jnp.float32)).astype(
        jnp.bfloat16
    )
    gathered = lax.all_gather(scaled, "row", axis=0, tiled=True)
    feature_tiles = gathered.reshape(col_tiles, tile_size, feat_width)
    list_length = packed.shape[0]

    def product_step(block_step, partial_value):
        logical = block_step * block_tiles + lane_index
        is_live = logical < live_count
        is_upper = logical >= live_count
        source = jnp.where(is_upper, logical - live_count, logical)
        source = jnp.clip(source, 0, list_length - 1)
        slot_number = jnp.minimum(is_upper.astype(jnp.int32), 1 - 1)
        tile_block = jnp.take(packed, source, axis=0)
        tile_block = jnp.where(is_live[:, None, None], tile_block, jnp.zeros((), jnp.bfloat16))
        inputs = jnp.take(feature_tiles, jnp.take(own_cols, source), axis=0)
        products = jnp.einsum(
            "bpq,bqf->bpf", tile_block, inputs, preferred_element_type=jnp.float32
        )
        return partial_value.at[slot_number, jnp.take(own_rows, source)].add(products)

    product_blocks = (live_count + block_tiles - 1) // block_tiles
    initial = jnp.zeros((1, row_tiles, tile_size, feat_width), jnp.float32)
    partial_value = lax.fori_loop(jnp.int32(0), product_blocks, product_step, initial)
    own_sum = partial_value[0]
    row_part_flat = row_acc.reshape(row_tiles * tile_size)
    summed, degree_share = (
        lax.psum_scatter(
            own_sum.reshape(row_tiles * tile_size, feat_width),
            "col",
            scatter_dimension=0,
            tiled=True,
        ),
        lax.psum_scatter(row_part_flat, "col", scatter_dimension=0, tiled=True),
    )
    aggregated = (lax.rsqrt(1.0 + degree_share)[:, None] * summed).astype(jnp.bfloat16)
    preact = jnp.dot(aggregated, weight, preferred_element_type=jnp.float32) + bias
    logistic = jax.nn.sigmoid(preact)
    hidden = (preact * logistic).astype(jnp.bfloat16)
    preact_grad = (
        cotangent.astype(jnp.float32) * logistic * (1.0 + preact * (1.0 - logistic))
    ).astype(jnp.bfloat16)
    weight_part = jnp.einsum(
        "nf,nh->fh", aggregated, preact_grad, preferred_element_type=jnp.float32
    )
    bias_part = jnp.sum(preact_grad.astype(jnp.float32), axis=0)
    weight_sum, bias_sum = lax.psum((weight_part, bias_part), ("row", "col"))
    inverse_root = lax.rsqrt(jnp.float32(summed.shape[0] * row_count * col_count))
    return (hidden, weight_sum * inverse_root, bias_sum * inverse_root)


def solution(mesh):
    placed = (
        P(("col", "row"), None),
        P(),
        P(),
        P(("row", "col"), None),
        P("row", "col", None, None, None),
        P("row", "col", None, None),
        P("row", "col"),
        P(),
    )
    return jax.shard_map(
        body,
        mesh=mesh,
        in_specs=placed,
        out_specs=(P(("row", "col"), None), P(), P()),
        check_vma=False,
    )
```

profile of v0, /device:TPU:1, one launch (start us, length us, event | category | flops | bytes accessed | tf_op | source)
XLA Modules:
  0.0 716.5 jit_solution(14614431443404107920)
XLA Ops:
  8.7 2.0 gather_fusion.8
  10.7 2.0 gather_fusion.7
  12.7 18.9 %while.24 = (s32[]{:T(128)}, f32[8,128]{1,0:T(8,128)S(1)}, f32[32,128]{1,0:T(8,128)S(1)}, s32[]{:T(128)}, s32[256]{0:T(256)S(1)}, /*index=5*/s32[]{:T(128)}, bf1...) while((s32[]{:T(128)}, f32[8,128]{1,0:T(8,128)S(1)}, ...), condition=%wide.region_5.9_spmd.clone, body=%wide.region_0.8_spmd.clone.sunk | while | flops 4213635 | bytes 6451793 | solution.py:44
  15.0 4.3 gather_fusion.2
  21.2 1.0 scatter_custom_fusion.16
  24.5 4.3 gather_fusion.2
  31.7 114.1 %all-reduce.1 = f32[4096]{0:T(1024)S(1)} all-reduce(f32[4096]{0:T(1024)S(1)} %bitcast.44), channel_id=3, replica_groups=mesh['row'=32,'col'=8] {'row'}, use_global_device_ids=true, to_apply=%region_7.11.clone | all-reduce | flops 4096 | bytes 32768
  147.9 70.0 %all-gather.2.cloned.1.call-done = bf16[4096,128]{1,0:T(8,128)(2,1)} async-done(((bf16[128,128]{1,0:T(8,128)(2,1)}), bf16[4096,128]{1,0:T(8,128)(2,1)}) %all-gather.2.cloned.1.call-update) | async-done | bytes 1048592 | tf_op jit(solution)/shard_map/all_gather | solution.py:58
  217.9 48.1 %while.25 = (s32[]{:T(128)}, f32[1,8,128,128]{3,2,1,0:T(8,128)S(1)}, s32[]{:T(128)}, s32[]{:T(128)}, s32[256]{0:T(256)S(1)}, /*index=5*/bf16[256,128,128]{2,1,0:...) while((s32[]{:T(128)}, f32[1,8,128,128]{3,2,1,0:T(8,128)S(1)}, ...), condition=%wide.region_10.14_spmd.clone, body=%wide.region_8.13_spmd.clone.sunk | while | flops 272634240 | bytes 41956408 | solution.py:79
  221.0 2.2 gather_fusion.6
  223.1 5.7 gather_fusion.4
  228.8 4.3 fusion.45
  233.1 8.8 %scatter_fusion = f32[8,128,128]{2,1,0:T(8,128)S(1)} fusion(f32[8,128,128]{2,1,0:T(8,128)S(1)} %bitcast.39, s32[64]{0:T(128)S(1)} %fusion.44, f32[64,128,128]{2,1,0:T(8,128)} %fusion.45), kind=kCustom, calls=%fused_computation.11.clone.clone.1 | custom fusion | flops 1048576 | bytes 12583168 | tf_op jit(solution)/shard_map/while/body/scatter-add | solution.py:75
  245.0 2.2 gather_fusion.6
  247.2 5.7 gather_fusion.4
  252.8 4.3 fusion.45
  257.2 8.8 %scatter_fusion = f32[8,128,128]{2,1,0:T(8,128)S(1)} fusion(f32[8,128,128]{2,1,0:T(8,128)S(1)} %bitcast.39, s32[64]{0:T(128)S(1)} %fusion.44, f32[64,128,128]{2,1,0:T(8,128)} %fusion.45), kind=kCustom, calls=%fused_computation.11.clone.clone.1 | custom fusion | flops 1048576 | bytes 12583168 | tf_op jit(solution)/shard_map/while/body/scatter-add | solution.py:75
  268.1 68.1 %all-reduce = f32[1024]{0:T(1024)S(1)} all-reduce(f32[1024]{0:T(1024)S(1)} %bitcast.45), channel_id=2, replica_groups=mesh['row'=32,'col'=8] {'col'}, use_global_device_ids=true, to_apply=%region_6.10.clone | all-reduce | flops 1024 | bytes 8192
  336.3 50.2 %reduce-scatter.2.cloned.1.call-done = f32[128,128]{1,0:T(8,128)} async-done(((f32[1024,128]{1,0:T(8,128)}), f32[128,128]{1,0:T(8,128)}) %reduce-scatter.2.cloned.1.call-update) | async-done | bytes 65552 | tf_op jit(solution)/shard_map/reduce_scatter | solution.py:83
  386.4 1.7 convert_reduce_fusion.2
  388.2 77.4 %psum.15 = f32[256]{0:T(256)S(1)} all-reduce(f32[256]{0:T(256)S(1)} %get-tuple-element.182), channel_id=1, replica_groups=mesh['row'=32,'col'=8] {'row','col'}, use_global_device_ids=true, to_apply=%region_14.18 | all-reduce | flops 256 | bytes 2048 | tf_op jit(solution)/shard_map/psum | solution.py:102
  465.6 1.8 fusion.33
  468.0 240.5 %all-reduce.4.cloned.1.call-done = f32[128,256]{1,0:T(8,128)} async-done(((f32[128,256]{1,0:T(8,128)}), f32[128,256]{1,0:T(8,128)}) %all-reduce.4.cloned.1.call-update) | async-done | bytes 131088 | tf_op jit(solution)/shard_map/psum | solution.py:102
  708.4 1.6 broadcast_multiply_fusion
  (74 shorter events, 19.6 us)
Async XLA Ops:
  7.2 379.3 %copy-start = (bf16[128,256]{1,0:T(8,128)(2,1)S(1)}, bf16[128,256]{1,0:T(8,128)(2,1)}, u32[]{:S(2)}) copy-start(bf16[128,256]{1,0:T(8,128)(2,1)} %param.19) | copy-start | bytes 196612
  7.2 210.6 %all-gather.2.cloned.1.call-start = ((), (), s32[]{:S(2)}) async-start(), calls=%async_computation.1 | async-start | bytes 1081344 | tf_op jit(solution)/shard_map/all_gather | solution.py:58
  12.7 133.1 %copy-start.8 = (u32[256]{0:T(256)S(1)}, u32[256]{0:T(256)}, u32[]{:S(2)}) copy-start(u32[256]{0:T(256)} %constant.133) | copy-start | bytes 3076
  12.7 134.4 %copy-start.4 = (bf16[128,128]{1,0:T(8,128)(2,1)S(1)}, bf16[128,128]{1,0:T(8,128)(2,1)}, u32[]{:S(2)}) copy-start(bf16[128,128]{1,0:T(8,128)(2,1)} %param.18) | copy-start | bytes 98308
  12.7 373.7 %copy-start.5 = (bf16[128,256]{1,0:T(8,128)(2,1)S(1)}, bf16[128,256]{1,0:T(8,128)(2,1)}, u32[]{:S(2)}) copy-start(bf16[128,256]{1,0:T(8,128)(2,1)} %param.21) | copy-start | bytes 196612
  147.8 238.6 %reduce-scatter.2.cloned.1.call-start = ((), (), s32[]{:S(2)}) async-start(), calls=%async_computation.2 | async-start | bytes 589824 | tf_op jit(solution)/shard_map/reduce_scatter | solution.py:83
  217.9 49.0 %copy-start.7 = (u32[256]{0:T(256)S(1)}, u32[256]{0:T(256)}, u32[]{:S(2)}) copy-start(u32[256]{0:T(256)} %constant.129) | copy-start | bytes 3076
  217.9 168.6 %copy-start.6 = (f32[256]{0:T(256)S(1)}, f32[256]{0:T(256)}, u32[]{:S(2)}) copy-start(f32[256]{0:T(256)} %param.20) | copy-start | bytes 3076
  217.9 3.1 copy-start.2
  223.1 5.7 copy-start.3
  241.9 3.1 copy-start.2
  247.2 5.7 copy-start.3
  266.0 0.8 copy-start.1
  266.8 441.7 %all-reduce.4.cloned.1.call-start = ((), (), s32[]{:S(2)}) async-start(), calls=%async_computation.3 | async-start | bytes 262144 | tf_op jit(solution)/shard_map/psum | solution.py:102
Sparse Core Ops, SparseCore 0:
  147.9 69.8 all-gather.1
  266.9 119.4 reduce-scatter.1
  467.5 240.8 all-reduce.3
where the time goes:
time: 718 us; the launch traced here: 717 us
  waiting for transfers between devices  361 us (50%)
  blocking collectives  260 us (36%)
  local copies, waits for them, and re-layouts  36.7 us (5%)
  other arithmetic  31.2 us (4%)
  between operations  15.9 us (2%)
  matrix products  12.1 us (2%)
    psum x1, waiting for transfers between devices, body(): weight_sum, bias_sum = lax.psum((weight_part, bias_part), ('row', 'col'))  240 us
    unnamed x2, blocking collectives  182 us
    psum x1, blocking collectives, body(): weight_sum, bias_sum = lax.psum((weight_part, bias_part), ('row', 'col'))  77.4 us
    all_gather x1, waiting for transfers between devices, body(): gathered = lax.all_gather(scaled, 'row', axis=0, tiled=True)  70 us
    reduce_scatter x1, waiting for transfers between devices, body(): lax.psum_scatter(own_sum.reshape(row_tiles * tile_size, feat_width), 'col...  50.2 us
    scatter-add x2, other arithmetic, product_step(): partial_value.at[slot_number, jnp.take(own_rows, source)].add(products)  17.6 us
  transfers between devices with their start and end apart: 3, of which 3 were waited for; matrix products, arithmetic and copies ran while one was open for 0% of the time, Pallas kernels for 0%

commit v1 on v0

v1 whole, which is shorter than its diff:
```python
import functools

import jax
import jax.numpy as jnp
from jax import lax
from jax.experimental import pallas as pl
from jax.experimental.pallas import tpu as pltpu
from jax.sharding import Mesh, PartitionSpec as P

ROW = ("z", "y_lo", "core")
COL = ("y_hi", "x")
SAME_CORE_ROW = ("z", "y_lo")
PLANE = ("y_lo", "core", "y_hi", "x")
SWAP = [(0, 1), (1, 0)]
CHUNK = 32
F32 = jnp.float32


def degree_kernel(ids, perm, count, pos, tiles, col_ref, slot_ref, acc):
    step = pl.program_id(0)
    row, col, core = ids[0], ids[1], ids[2]
    live_count = count[0, 0]

    @pl.when(step == 0)
    def _():
        acc[...] = jnp.zeros_like(acc)

        @pl.loop(0, 264)
        def _(n):
            slot_ref[n] = jnp.int32(-1)

    @pl.when(step * CHUNK < live_count)
    def _():
        @pl.loop(0, CHUNK // 8)
        def _(group):
            for u in range(8):
                local = group * 8 + u
                slot = step * CHUNK + local
                own_row = perm[row * 8 + pos[0, slot]] - row * 8
                own_col = perm[col * 32 + pos[1, slot]] - col * 32
                place = (own_col >> 1) + 16 * ((own_col & 1) ^ core)
                live = slot < live_count
                slot_ref[jnp.where(live, own_row * 32 + place, 256)] = slot
                part = jnp.sum(tiles[local].astype(F32).reshape(16, 8, 128), axis=0)
                acc[place] += jnp.where(live, part, 0.0)

    @pl.when(step == pl.num_programs(0) - 1)
    def _():
        col_ref[...] = jnp.sum(acc[...], axis=1)


def degrees(ids, perm, count, pos, packed):
    steps = packed.shape[0] // CHUNK

    def block(step, ids, perm, count, pos):
        last = jnp.maximum(count[0, 0] - 1, 0) // CHUNK
        return (jnp.minimum(step, last), 0, 0)

    return pl.pallas_call(
        degree_kernel,
        grid_spec=pltpu.PrefetchScalarGridSpec(
            num_scalar_prefetch=4,
            grid=(steps,),
            in_specs=[pl.BlockSpec((CHUNK, 128, 128), block)],
            out_specs=[
                pl.BlockSpec((32, 128), lambda step, *_: (0, 0)),
                pl.BlockSpec(memory_space=pltpu.SMEM),
            ],
            scratch_shapes=[pltpu.VMEM((32, 8, 128), F32)],
        ),
        out_shape=[
            jax.ShapeDtypeStruct((32, 128), F32),
            jax.ShapeDtypeStruct((264,), jnp.int32),
        ],
        name="degrees",
    )(ids, perm, count, pos, packed)


def product_kernel(slots, deg, feat_a, feat_b, *refs):
    tiles, (out, rhs) = refs[:32], refs[32:]
    i = pl.program_id(0)

    @pl.when(i == 0)
    def _():
        scale = jnp.concatenate([lax.rsqrt(1.0 + deg[...]), jnp.zeros((96, 128), F32)], axis=0).T
        for b in range(32):
            feat = feat_a[b] if b < 16 else feat_b[b - 16]
            scaled = scale[:, b : b + 1] * feat.astype(F32)
            rhs[pl.ds(b * 128, 128), 0:128] = scaled.astype(jnp.bfloat16)
            rhs[pl.ds(b * 128, 128), 128:256] = jnp.ones((128, 128), jnp.bfloat16)

    parts = []
    for q in range(32):
        live = slots[i * 32 + q] >= 0
        parts.append(jnp.where(live, tiles[q][0], jnp.zeros((), jnp.bfloat16)))
    lhs = jnp.concatenate(parts, axis=1)
    both = jnp.dot(lhs, rhs[...], preferred_element_type=F32)
    out[0, 0:128, :] = both[:, 0:128]
    out[0, 128:136, :] = both[:, 128:256].T[0:8, :]


def product(slots, deg, feat_a, feat_b, packed):
    def block(q, i, slots):
        return (jnp.maximum(slots[i * 32 + q], 0), 0, 0)

    whole = pl.BlockSpec((16, 128, 128), lambda i, slots: (0, 0, 0))
    return pl.pallas_call(
        product_kernel,
        grid_spec=pltpu.PrefetchScalarGridSpec(
            num_scalar_prefetch=1,
            grid=(8,),
            in_specs=[pl.BlockSpec((32, 128), lambda i, slots: (0, 0)), whole, whole]
            + [pl.BlockSpec((1, 128, 128), functools.partial(block, q)) for q in range(32)],
            out_specs=pl.BlockSpec((1, 136, 128), lambda i, slots: (i, 0, 0)),
            scratch_shapes=[pltpu.VMEM((4096, 256), jnp.bfloat16)],
        ),
        out_shape=jax.ShapeDtypeStruct((8, 136, 128), F32),
        name="product",
    )(slots, deg, feat_a, feat_b, *([packed] * 32))


def node_kernel(parts, weight, bias, cotangent, hidden_ref, terms_ref):
    total = jnp.sum(parts[...], axis=0)
    row_degree = jnp.broadcast_to(1.0 + total[128:129, :], (128, 128)).T
    aggregated = (lax.rsqrt(row_degree) * total[0:128, :]).astype(jnp.bfloat16)
    preact = jnp.dot(aggregated, weight[...], preferred_element_type=F32) + bias[...]
    logistic = jax.nn.sigmoid(preact)
    hidden_ref[...] = (preact * logistic).astype(jnp.bfloat16)
    grad = (
        cotangent[...].astype(F32) * logistic * (1.0 + preact * (1.0 - logistic))
    ).astype(jnp.bfloat16)
    weight_part = lax.dot_general(
        aggregated, grad, (((0,), (0,)), ((), ())), preferred_element_type=F32
    )
    bias_part = jnp.sum(grad.astype(F32), axis=0, keepdims=True)
    for k in range(32):
        half, f = k // 16, (k % 16) * 8
        for s in range(8):
            terms_ref[k, s, :, :] = weight_part[f + s : f + s + 1, half * 128 : half * 128 + 128]
        terms_ref[k, 8, :, :] = (
            bias_part[:, k * 128 : k * 128 + 128] if k < 2 else jnp.zeros((1, 128), F32)
        )


def nodes(parts, weight, bias, cotangent):
    return pl.pallas_call(
        node_kernel,
        out_shape=[
            jax.ShapeDtypeStruct((128, 256), jnp.bfloat16),
            jax.ShapeDtypeStruct((32, 9, 1, 128), F32),
        ],
        name="nodes",
    )(parts, weight, bias, cotangent)


def gather(x, axes, count):
    return lax.all_to_all(jnp.broadcast_to(x[None], (count,) + x.shape), axes, 0, 0)


def body(features, weight, bias, cotangent, tile_values, tile_pos, tile_count, block_perm):
    packed = tile_values[0, 0]
    ids = jnp.stack([lax.axis_index(ROW), lax.axis_index(COL), lax.axis_index("core")])
    feat_a = gather(features, SAME_CORE_ROW, 16)
    col_part, slots = degrees(ids, block_perm, tile_count, tile_pos[0, 0], packed)
    col_half = col_part[:16] + lax.ppermute(col_part[16:], "core", SWAP)
    deg_a = jnp.sum(gather(col_half, SAME_CORE_ROW, 16), axis=0)
    deg_b = lax.ppermute(deg_a, "core", SWAP)
    feat_b = lax.ppermute(feat_a, "core", SWAP)
    partial = product(slots, jnp.concatenate([deg_a, deg_b]), feat_a, feat_b, packed)
    received = lax.all_to_all(partial, COL, 0, 0)
    hidden, terms = nodes(received, weight, bias[None], cotangent)
    own_terms = jnp.sum(lax.all_to_all(terms, PLANE, 0, 0), axis=0)
    total = jnp.sum(gather(own_terms, ("z",), 8), axis=0) * lax.rsqrt(F32(32768.0))
    every = gather(total, PLANE, 32)[:, :, 0, :]
    weight_rows = every[:, :8, :].reshape(2, 128, 128)
    weight_grad = jnp.concatenate([weight_rows[0], weight_rows[1]], axis=1)
    return hidden, weight_grad, every[:2, 8, :].reshape(256)


def solution(mesh):
    split = Mesh(mesh.devices.reshape(8, 2, 2, 2, 4), ("z", "y_lo", "core", "y_hi", "x"))
    placed = (
        P(COL + ROW, None),
        P(),
        P(),
        P(ROW + COL, None),
        P(ROW, COL, None, None, None),
        P(ROW, COL, None, None),
        P(ROW, COL),
        P(),
    )
    return jax.shard_map(
        body,
        mesh=split,
        in_specs=placed,
        out_specs=(P(ROW + COL, None), P(), P()),
        check_vma=False,
    )
```

time: 718 us -> 118 us (0.16)
  waiting for transfers between devices: 361 us -> 7.05 us
  blocking collectives: 260 us -> 64.9 us
  local copies, waits for them, and re-layouts: 36.7 us -> 3.9 us
  other arithmetic: 31.2 us -> 2.75 us
  Pallas kernels: 0 us -> 22.5 us
  between operations: 15.9 us -> 1.36 us
  starting transfers between devices: 0.12 us -> 14.6 us
  matrix products: 12.1 us -> 0 us
    psum x1 -> x0, waiting for transfers between devices: 240 us -> none  [body(): weight_sum, bias_sum = lax.psum((weight_part, bias_part), ('row', 'col'))]
    unnamed x2 -> x0, blocking collectives: 182 us -> none
    psum x1 -> x0, blocking collectives: 77.4 us -> none  [body(): weight_sum, bias_sum = lax.psum((weight_part, bias_part), ('row', 'col'))]
    all_gather x1 -> x0, waiting for transfers between devices: 70 us -> none  [body(): gathered = lax.all_gather(scaled, 'row', axis=0, tiled=True)]
    all_to_all x0 -> x5, blocking collectives: none -> 64.9 us  [the longest x3 33.5 us: gather(): lax.all_to_all(jnp.broadcast_to(x[None], (count,) + x.shape), axes, 0, 0)]
    reduce_scatter x1 -> x0, waiting for transfers between devices: 50.2 us -> none  [body(): lax.psum_scatter(own_sum.reshape(row_tiles * tile_size, feat_width), 'col...]
    gather x16 -> x0, local copies, waits for them, and re-layouts: 34.6 us -> none  [the longest x2 11.3 us: product_step(): tile_block = jnp.take(packed, source, axis=0)]
    pallas_call x0 -> x3, Pallas kernels: none -> 22.5 us  [the longest x1 12.8 us: product(): pl.pallas_call(product_kernel, grid_spec=pltpu.PrefetchScalarGridSpec(num...]
  transfers between devices with their start and end apart: 3 -> 4, of which waited for: 3 -> 2; matrix products, arithmetic and copies ran while one was open for 0% -> 2% of each run, Pallas kernels for 0% -> 6%
where the time goes in v1:
time: 118 us; the launch traced here: 117 us
  blocking collectives  64.9 us (55%)
  Pallas kernels  22.5 us (19%)
  starting transfers between devices  14.6 us (12%)
  waiting for transfers between devices  7.05 us (6%)
  local copies, waits for them, and re-layouts  3.9 us (3%)
  other arithmetic  2.75 us (2%)
  between operations  1.36 us (1%)
    all_to_all x3, blocking collectives, gather(): lax.all_to_all(jnp.broadcast_to(x[None], (count,) + x.shape), axes, 0, 0)  33.5 us
    all_to_all x1, blocking collectives, body(): received = lax.all_to_all(partial, COL, 0, 0)  18.9 us
    pallas_call x1, Pallas kernels, product(): pl.pallas_call(product_kernel, grid_spec=pltpu.PrefetchScalarGridSpec(num...  12.8 us
    all_to_all x1, blocking collectives, body(): own_terms = jnp.sum(lax.all_to_all(terms, PLANE, 0, 0), axis=0)  12.5 us
    all_to_all x1, starting transfers between devices, gather(): lax.all_to_all(jnp.broadcast_to(x[None], (count,) + x.shape), axes, 0, 0)  10.1 us
    pallas_call x1, Pallas kernels, degrees(): pl.pallas_call(degree_kernel, grid_spec=pltpu.PrefetchScalarGridSpec(num_...  7.5 us
    all_to_all x1, waiting for transfers between devices, gather(): lax.all_to_all(jnp.broadcast_to(x[None], (count,) + x.shape), axes, 0, 0)  6.21 us
    ppermute x1, starting transfers between devices, body(): feat_b = lax.ppermute(feat_a, 'core', SWAP)  2.56 us
  transfers between devices with their start and end apart: 4, of which 2 were waited for; matrix products, arithmetic and copies ran while one was open for 2% of the time, Pallas kernels for 6%

profile of v1, /device:TPU:1, one launch (start us, length us, event | category | flops | bytes accessed | tf_op | source)
XLA Modules:
  0.0 117.1 jit_solution(3412071247813578997)
XLA Ops:
  0.6 1.7 %broadcast_in_dim.11 = bf16[16,128,128]{2,1,0:T(8,128)(2,1)} broadcast(bf16[128,128]{1,0:T(8,128)(2,1)} %param.8), dimensions={1,2} | broadcast | bytes 557056 | tf_op jit(solution)/shard_map/broadcast_in_dim | solution.py:157
  2.3 10.1 %all-to-all-start.1 = ((bf16[16,128,128]{2,1,0:T(8,128)(2,1)}), bf16[16,128,128]{2,1,0:T(8,128)(2,1)S(1)}, u32[]{:S(2)}, u32[]{:S(2)}) async-start(bf16[16,128,128]{2,1,0:T(8,128)(2,1)} %broadcast_in_dim.11), calls=%async_computation.1 | async-start | bytes 1048576 | tf_op jit(solution)/shard_map/all_to_all | solution.py:157
  13.1 0.6 pad_add_fusion.ids
  13.7 7.5 %degrees.1 = (f32[32,128]{1,0:T(8,128)}, s32[264]{0:T(512)}) custom-call(s32[3]{0:T(128)} %pad_add_fusion.ids, s32[256]{0:T(256)} %perm.1, s32[1,1]{1,0:T(1,128)S(6)} %copy.27.count, s32[2,256]{1,0:T(2,128)} %bitcast.50, bf16[256,128,128]{2,1,0:T(8,128)(2,1)} %bitcast.15), custom_call_target="tpu_custom_call" | custom-call | tf_op jit(solution)/shard_map/degrees/pallas_call | solution.py:59
  21.2 0.7 slice.21
  21.9 6.2 %all-to-all-done.1.feat_a = bf16[16,128,128]{2,1,0:T(8,128)(2,1)S(1)} async-done(((bf16[16,128,128]{2,1,0:T(8,128)(2,1)}), bf16[16,128,128]{2,1,0:T(8,128)(2,1)S(1)}, u32[]{:S(2)}, u32[]{:S(2)}) %all-to-all-start.1) | async-done | bytes 524320 | tf_op jit(solution)/shard_map/all_to_all | solution.py:157
  28.1 2.6 %collective-permute-start.2 = (bf16[16,128,128]{2,1,0:T(8,128)(2,1)S(1)}, bf16[16,128,128]{2,1,0:T(8,128)(2,1)S(1)}, u32[]{:S(2)}, u32[]{:S(2)}) collective-permute-start(bf16[16,128,128]{2,1,0:T(8,128)(2,1)S(1)} %all-to-all-done.1.feat_a), channel_id=1, source_target_pairs={{0,8},{8,0},{1,9},{9,1},{2,10},{10,2},{3,11},{11,3},{4,12},{12,4},... | collective-permute-start | bytes 1572872 | tf_op jit(solution)/shard_map/ppermute | solution.py:168
  30.7 0.0 collective-permute-done
  30.7 0.7 slice_add_fusion
  31.4 11.4 %all_to_all.30 = f32[16,16,128]{2,1,0:T(8,128)S(1)} all-to-all(f32[16,16,128]{2,1,0:T(8,128)S(1)} %broadcast_in_dim.10), channel_id=1, replica_groups=mesh['z'=8,'y_lo'=2,'core'=2,'y_hi'=2,'x'=4] {'z','y_lo'}, dimensions={0} | all-to-all | bytes 262144 | tf_op jit(solution)/shard_map/all_to_all | solution.py:157
  42.8 2.0 %collective-permute-start.1 = (f32[16,128]{1,0:T(8,128)S(1)}, f32[16,128]{1,0:T(8,128)S(1)}, u32[]{:S(2)}, u32[]{:S(2)}) collective-permute-start(f32[16,128]{1,0:T(8,128)S(1)} %reduce_sum.27), channel_id=1, source_target_pairs={{0,8},{8,0},{1,9},{9,1},{2,10},{10,2},{3,11},{11,3},{4,12},{12,4},... | collective-permute-start | bytes 24584 | tf_op jit(solution)/shard_map/ppermute | solution.py:167
  44.8 0.8 collective-permute-done.1
  45.6 0.6 pad_maximum_fusion.1.deg
  46.2 0.8 copy-done.1
  47.0 12.8 %product.1 = f32[8,136,128]{2,1,0:T(8,128)} custom-call(s32[264]{0:T(512)} %get-tuple-element.7.slots, f32[32,128]{1,0:T(8,128)} %pad_maximum_fusion.1.deg, bf16[16,128,128]{2,1,0:T(8,128)(2,1)} %copy-done, bf16[16,128,128]{2,1,0:T(8,128)(2,1)} %copy-done.1, bf16[256,128,128]{2,1,0:T(8,128)(2,1)} %bitcast.31, bf16[256,128,128]{2,1,0:T(8,128)(2,1)} %bitcast.47, ...), custom_call_target="tpu_custom_call" | custom-call | tf_op jit(solution)/shard_map/product/pallas_call | solution.py:107
  59.8 18.9 %all_to_all.31.parts = f32[8,136,128]{2,1,0:T(8,128)} all-to-all(f32[8,136,128]{2,1,0:T(8,128)} %product.1), channel_id=1, replica_groups=mesh['z'=8,'y_lo'=2,'core'=2,'y_hi'=2,'x'=4] {'y_hi','x'}, dimensions={0} | all-to-all | bytes 1114112 | tf_op jit(solution)/shard_map/all_to_all | solution.py:170
  78.7 2.2 %nodes.1 = (bf16[128,256]{1,0:T(8,128)(2,1)}, f32[32,9,1,128]{3,2,1,0:T(1,128)}) custom-call(f32[8,136,128]{2,1,0:T(8,128)} %all_to_all.31.parts, bf16[128,256]{1,0:T(8,128)(2,1)} %weight.1, f32[1,256]{1,0:T(1,128)} %bitcast.51, bf16[128,256]{1,0:T(8,128)(2,1)} %cotangent.1), custom_call_target="tpu_custom_call" | custom-call | tf_op jit(solution)/shard_map/nodes/pallas_call | solution.py:146
  80.9 12.5 %all_to_all.32 = f32[32,9,1,128]{3,2,1,0:T(1,128)S(1)} all-to-all(f32[32,9,1,128]{3,2,1,0:T(1,128)} %get-tuple-element.10), channel_id=1, replica_groups=mesh['z'=8,'y_lo'=2,'core'=2,'y_hi'=2,'x'=4] {'y_lo','core','y_hi','x'}, dimensions={0} | all-to-all | bytes 294912 | tf_op jit(solution)/shard_map/all_to_all | solution.py:172
  93.4 0.1 reduce_sum.28
  93.6 9.4 %all_to_all.33 = f32[8,9,1,128]{3,2,1,0:T(1,128)S(1)} all-to-all(f32[8,9,1,128]{3,2,1,0:T(1,128)S(1)} %broadcast_in_dim.13), channel_id=1, replica_groups=mesh['z'=8,'y_lo'=2,'core'=2,'y_hi'=2,'x'=4] {'z'}, dimensions={0} | all-to-all | bytes 73728 | tf_op jit(solution)/shard_map/all_to_all | solution.py:157
  103.0 0.1 broadcast_in_dim.14
  103.1 12.7 %all_to_all.34 = f32[32,9,1,128]{3,2,1,0:T(1,128)S(1)} all-to-all(f32[32,9,1,128]{3,2,1,0:T(1,128)S(1)} %broadcast_in_dim.14), channel_id=1, replica_groups=mesh['z'=8,'y_lo'=2,'core'=2,'y_hi'=2,'x'=4] {'y_lo','core','y_hi','x'}, dimensions={0} | all-to-all | bytes 294912 | tf_op jit(solution)/shard_map/all_to_all | solution.py:157
  115.8 0.6 slice_bitcast_fusion
  116.4 0.7 pad_maximum_fusion
  (13 shorter events, 0.2 us)
Async XLA Ops:
  2.3 25.8 %all-to-all-start.1 = ((bf16[16,128,128]{2,1,0:T(8,128)(2,1)}), bf16[16,128,128]{2,1,0:T(8,128)(2,1)S(1)}, u32[]{:S(2)}, u32[]{:S(2)}) async-start(bf16[16,128,128]{2,1,0:T(8,128)(2,1)} %broadcast_in_dim.11), calls=%async_computation.1 | async-start | bytes 1048576 | tf_op jit(solution)/shard_map/all_to_all | solution.py:157
  21.9 8.8 %collective-permute-start = (f32[16,128]{1,0:T(8,128)S(1)}, f32[16,128]{1,0:T(8,128)S(1)}, u32[]{:S(2)}, u32[]{:S(2)}) collective-permute-start(f32[16,128]{1,0:T(8,128)S(1)} %slice.21), channel_id=1, source_target_pairs={{0,8},{8,0},{1,9},{9,1},{2,10},{10,2},{3,11},{11,3},{4,12},{12,4},... | collective-permute-start | bytes 24584 | tf_op jit(solution)/shard_map/ppermute | solution.py:165
  28.1 18.1 %copy-start = (bf16[16,128,128]{2,1,0:T(8,128)(2,1)}, bf16[16,128,128]{2,1,0:T(8,128)(2,1)S(1)}, u32[]{:S(2)}) copy-start(bf16[16,128,128]{2,1,0:T(8,128)(2,1)S(1)} %all-to-all-done.1.feat_a) | copy-start | bytes 1572868
  28.1 18.1 %collective-permute-start.2 = (bf16[16,128,128]{2,1,0:T(8,128)(2,1)S(1)}, bf16[16,128,128]{2,1,0:T(8,128)(2,1)S(1)}, u32[]{:S(2)}, u32[]{:S(2)}) collective-permute-start(bf16[16,128,128]{2,1,0:T(8,128)(2,1)S(1)} %all-to-all-done.1.feat_a), channel_id=1, source_target_pairs={{0,8},{8,0},{1,9},{9,1},{2,10},{10,2},{3,11},{11,3},{4,12},{12,4},... | collective-permute-start | bytes 1572872 | tf_op jit(solution)/shard_map/ppermute | solution.py:168
  42.8 2.8 %collective-permute-start.1 = (f32[16,128]{1,0:T(8,128)S(1)}, f32[16,128]{1,0:T(8,128)S(1)}, u32[]{:S(2)}, u32[]{:S(2)}) collective-permute-start(f32[16,128]{1,0:T(8,128)S(1)} %reduce_sum.27), channel_id=1, source_target_pairs={{0,8},{8,0},{1,9},{9,1},{2,10},{10,2},{3,11},{11,3},{4,12},{12,4},... | collective-permute-start | bytes 24584 | tf_op jit(solution)/shard_map/ppermute | solution.py:167
  46.2 0.8 copy-start.1

commit v2 on v1

v2 whole, which is shorter than its diff:
```python
import functools

import jax
import jax.numpy as jnp
from jax import lax
from jax.experimental import pallas as pl
from jax.experimental.pallas import tpu as pltpu
from jax.sharding import Mesh, PartitionSpec as P

ROW = ("z", "y_lo", "core")
COL = ("y_hi", "x")
SAME_CORE_ROW = ("z", "y_lo")
PLANE = ("y_lo", "core", "y_hi", "x")
SWAP = [(0, 1), (1, 0)]
CHUNK = 32
F32 = jnp.float32
BF16 = jnp.bfloat16


def degree_kernel(count, perm, pos, feats, tiles, send_ref, slot_ref, sums):
    step = pl.program_id(0)
    live_count = count[0, 0]

    @pl.when(step * CHUNK < live_count)
    def _():
        for group in range(CHUNK // 8):
            rows = []
            for u in range(8):
                tile = tiles[group * 8 + u].astype(F32)
                rows.append(jnp.sum(tile, axis=0, keepdims=True))
            sums[pl.ds(step * CHUNK + group * 8, 8), :] = jnp.concatenate(rows, axis=0)

    @pl.when(step * CHUNK >= live_count)
    def _():
        sums[pl.ds(step * CHUNK, CHUNK), :] = jnp.zeros((CHUNK, 128), F32)

    @pl.when(step == pl.num_programs(0) - 1)
    def _():
        row, col, core = lax.axis_index(ROW), lax.axis_index(COL), lax.axis_index("core")
        own_row = jnp.zeros((1, 256), jnp.int32)
        own_col = jnp.zeros((1, 256), jnp.int32)
        for v in range(8):
            own_row += jnp.where(pos[0:1, :] == v, perm[row * 8 + v] - row * 8, 0)
        for v in range(32):
            own_col += jnp.where(pos[1:2, :] == v, perm[col * 32 + v] - col * 32, 0)
        place = (own_col >> 1) + 16 * ((own_col & 1) ^ core)
        slot = lax.broadcasted_iota(jnp.int32, (1, 256), 1)
        live = slot < live_count
        place = jnp.where(live, place, 512)
        dense = own_row * 32 + place
        pick = (lax.broadcasted_iota(jnp.int32, (32, 256), 0) == place).astype(F32)
        col_part = jnp.dot(
            pick, sums[...], precision=lax.Precision.HIGHEST, preferred_element_type=F32
        ).astype(BF16)
        match = lax.broadcasted_iota(jnp.int32, (256, 256), 0) == dense
        number = lax.broadcasted_iota(jnp.int32, (16, 256), 1) + 1
        found = lax.dot_general(
            number.astype(F32).astype(BF16),
            match.astype(F32).astype(BF16),
            (((1,), (1,)), ((), ())),
            preferred_element_type=F32,
        )
        slot_ref[...] = found[0:1, :].astype(jnp.int32) - 1
        for m in range(16):
            send_ref[m, 0:128, :] = feats[...]
            send_ref[m, 128:160, :] = col_part


def degrees(count, perm, pos, features, packed):
    steps = packed.shape[0] // CHUNK

    def block(step, count, perm):
        last = jnp.maximum(count[0, 0] - 1, 0) // CHUNK
        return (jnp.minimum(step, last), 0, 0)

    return pl.pallas_call(
        degree_kernel,
        grid_spec=pltpu.PrefetchScalarGridSpec(
            num_scalar_prefetch=2,
            grid=(steps,),
            in_specs=[
                pl.BlockSpec((2, 256), lambda step, *_: (0, 0)),
                pl.BlockSpec((128, 128), lambda step, *_: (0, 0)),
                pl.BlockSpec((CHUNK, 128, 128), block),
            ],
            out_specs=[
                pl.BlockSpec((16, 160, 128), lambda step, *_: (0, 0, 0)),
                pl.BlockSpec((1, 256), lambda step, *_: (0, 0)),
            ],
            scratch_shapes=[pltpu.VMEM((256, 128), F32)],
        ),
        out_shape=[
            jax.ShapeDtypeStruct((16, 160, 128), BF16),
            jax.ShapeDtypeStruct((1, 256), jnp.int32),
        ],
        compiler_params=pltpu.CompilerParams(vmem_limit_bytes=16 << 20),
        name="degrees",
    )(count, perm, pos, features, packed)


def product_kernel(slots, recv_a, recv_b, tiles, out, rhs, acc):
    from_a = jnp.sum(recv_a[:, 128:160, :].astype(F32), axis=0)
    from_b = jnp.sum(recv_b[:, 128:160, :].astype(F32), axis=0)
    degree = 1.0 + from_a + jnp.concatenate([from_b[16:32], from_b[0:16]], axis=0)
    scale = jnp.concatenate([lax.rsqrt(degree), jnp.zeros((96, 128), F32)], axis=0).T
    for b in range(32):
        feat = recv_a[b, 0:128, :] if b < 16 else recv_b[b - 16, 0:128, :]
        scaled = scale[:, b : b + 1] * feat.astype(F32)
        rhs[pl.ds(b * 128, 128), 0:128] = scaled.astype(BF16)
    rhs[:, 128:256] = jnp.ones((4096, 128), BF16)
    acc[...] = jnp.zeros_like(acc)

    @pl.loop(0, 8)
    def _(s):
        rows = []
        for i in range(8):
            parts = []
            for q in range(4):
                slot = slots[0, i * 32 + s * 4 + q]
                tile = tiles[jnp.maximum(slot, 0)]
                parts.append(jnp.where(slot >= 0, tile, jnp.zeros((), BF16)))
            rows.append(jnp.concatenate(parts, axis=1))
        lhs = jnp.concatenate(rows, axis=0)
        acc[...] += jnp.dot(
            lhs, rhs[pl.ds(pl.multiple_of(s * 512, 512), 512), :], preferred_element_type=F32
        )

    for i in range(8):
        out[i, 0:128, :] = acc[i * 128 : i * 128 + 128, 0:128].astype(BF16)
        sums = acc[i * 128 : i * 128 + 128, 128:256].T[0:8, :]
        high = sums.astype(BF16)
        low = (sums - high.astype(F32)).astype(BF16)
        out[i, 128:144, :] = jnp.concatenate([high, low], axis=0)


def product(slots, recv_a, recv_b, packed):
    vmem = pl.BlockSpec(memory_space=pltpu.VMEM)
    return pl.pallas_call(
        product_kernel,
        in_specs=[pl.BlockSpec(memory_space=pltpu.SMEM), vmem, vmem, vmem],
        out_specs=vmem,
        scratch_shapes=[pltpu.VMEM((4096, 256), BF16), pltpu.VMEM((1024, 256), F32)],
        out_shape=jax.ShapeDtypeStruct((8, 144, 128), BF16),
        compiler_params=pltpu.CompilerParams(vmem_limit_bytes=24 << 20),
        name="product",
    )(slots, recv_a, recv_b, packed)


def node_kernel(parts, weight, bias, cotangent, hidden_ref, terms_ref):
    total = jnp.sum(parts[...].astype(F32), axis=0)
    row_degree = jnp.broadcast_to(1.0 + total[128:129, :] + total[136:137, :], (128, 128)).T
    aggregated = (lax.rsqrt(row_degree) * total[0:128, :]).astype(BF16)
    preact = jnp.dot(aggregated, weight[...], preferred_element_type=F32) + bias[...]
    logistic = jax.nn.sigmoid(preact)
    hidden_ref[...] = (preact * logistic).astype(BF16)
    grad = (
        cotangent[...].astype(F32) * logistic * (1.0 + preact * (1.0 - logistic))
    ).astype(BF16)
    weight_part = lax.dot_general(
        aggregated, grad, (((0,), (0,)), ((), ())), preferred_element_type=F32
    )
    bias_part = jnp.sum(grad.astype(F32), axis=0, keepdims=True)
    for k in range(32):
        half, f = k // 16, (k % 16) * 8
        for s in range(8):
            terms_ref[k, s, :, :] = weight_part[f + s : f + s + 1, half * 128 : half * 128 + 128]
        terms_ref[k, 8, :, :] = (
            bias_part[:, k * 128 : k * 128 + 128] if k < 2 else jnp.zeros((1, 128), F32)
        )


def nodes(parts, weight, bias, cotangent):
    return pl.pallas_call(
        node_kernel,
        out_shape=[
            jax.ShapeDtypeStruct((128, 256), BF16),
            jax.ShapeDtypeStruct((32, 9, 1, 128), F32),
        ],
        compiler_params=pltpu.CompilerParams(vmem_limit_bytes=16 << 20),
        name="nodes",
    )(parts, weight, bias, cotangent)


def gather(x, axes, count):
    return lax.all_to_all(jnp.broadcast_to(x[None], (count,) + x.shape), axes, 0, 0)


def body(features, weight, bias, cotangent, tile_values, tile_pos, tile_count, block_perm):
    packed = tile_values[0, 0]
    streamed = pltpu.with_memory_space_constraint(packed, pltpu.HBM)
    send, slots = degrees(tile_count, block_perm, tile_pos[0, 0], features, streamed)
    recv_a = lax.all_to_all(send, SAME_CORE_ROW, 0, 0)
    recv_b = lax.ppermute(recv_a, "core", SWAP)
    held = pltpu.with_memory_space_constraint(packed, pltpu.VMEM)
    partial = product(slots, recv_a, recv_b, held)
    received = lax.all_to_all(partial, COL, 0, 0)
    hidden, terms = nodes(received, weight, bias[None], cotangent)
    own_terms = jnp.sum(lax.all_to_all(terms, PLANE, 0, 0), axis=0)
    total = jnp.sum(gather(own_terms, ("z",), 8), axis=0) * lax.rsqrt(F32(32768.0))
    every = gather(total, PLANE, 32)[:, :, 0, :]
    weight_rows = every[:, :8, :].reshape(2, 128, 128)
    weight_grad = jnp.concatenate([weight_rows[0], weight_rows[1]], axis=1)
    return hidden, weight_grad, every[:2, 8, :].reshape(256)


def solution(mesh):
    split = Mesh(mesh.devices.reshape(8, 2, 2, 2, 4), ("z", "y_lo", "core", "y_hi", "x"))
    placed = (
        P(COL + ROW, None),
        P(),
        P(),
        P(ROW + COL, None),
        P(ROW, COL, None, None, None),
        P(ROW, COL, None, None),
        P(ROW, COL),
        P(),
    )
    return jax.shard_map(
        body,
        mesh=split,
        in_specs=placed,
        out_specs=(P(ROW + COL, None), P(), P()),
        check_vma=False,
    )
```

time: 118 us -> 99.1 us (0.84)
  Pallas kernels: 22.5 us -> 10.2 us
  blocking collectives: 64.9 us -> 76.3 us
  starting transfers between devices: 14.6 us -> 4.88 us
  waiting for transfers between devices: 7.05 us -> 1.72 us
  other arithmetic: 2.75 us -> 0.81 us
    all_to_all x0 -> x1, blocking collectives: none -> 25.6 us  [body(): recv_a = lax.all_to_all(send, SAME_CORE_ROW, 0, 0)]
    all_to_all x3 -> x2, blocking collectives: 33.5 us -> 22.1 us  [gather(): lax.all_to_all(jnp.broadcast_to(x[None], (count,) + x.shape), axes, 0, 0)]
    all_to_all x1 -> x0, starting transfers between devices: 10.1 us -> none  [gather(): lax.all_to_all(jnp.broadcast_to(x[None], (count,) + x.shape), axes, 0, 0)]
    pallas_call x2, Pallas kernels: 15 us -> 6.02 us  [the longest x1 5.13 us: product(): pl.pallas_call(product_kernel, in_specs=[pl.BlockSpec(memory_space=pltpu....]
    all_to_all x1 -> x0, waiting for transfers between devices: 6.21 us -> none  [gather(): lax.all_to_all(jnp.broadcast_to(x[None], (count,) + x.shape), axes, 0, 0)]
    pallas_call x1, Pallas kernels: 7.5 us -> 4.19 us  [degrees(): pl.pallas_call(degree_kernel, grid_spec=pltpu.PrefetchScalarGridSpec(num_...]
    all_to_all x1, blocking collectives: 18.9 us -> 17 us  [body(): received = lax.all_to_all(partial, COL, 0, 0)]
    unnamed x4 -> x14, local copies, waits for them, and re-layouts: 0.81 us -> 2.54 us
  transfers between devices with their start and end apart: 4 -> 1, of which waited for: 2 -> 1; matrix products, arithmetic and copies ran while one was open for 2% -> 0% of each run, Pallas kernels for 6% -> 0%
where the time goes in v2:
time: 99.1 us; the launch traced here: 98.7 us
  blocking collectives  76.3 us (77%)
  Pallas kernels  10.2 us (10%)
  starting transfers between devices  4.88 us (5%)
  local copies, waits for them, and re-layouts  3.27 us (3%)
  waiting for transfers between devices  1.72 us (2%)
  between operations  1.51 us (2%)
    all_to_all x1, blocking collectives, body(): recv_a = lax.all_to_all(send, SAME_CORE_ROW, 0, 0)  25.6 us
    all_to_all x2, blocking collectives, gather(): lax.all_to_all(jnp.broadcast_to(x[None], (count,) + x.shape), axes, 0, 0)  22.1 us
    all_to_all x1, blocking collectives, body(): received = lax.all_to_all(partial, COL, 0, 0)  17 us
    all_to_all x1, blocking collectives, body(): own_terms = jnp.sum(lax.all_to_all(terms, PLANE, 0, 0), axis=0)  11.6 us
    pallas_call x1, Pallas kernels, product(): pl.pallas_call(product_kernel, in_specs=[pl.BlockSpec(memory_space=pltpu....  5.13 us
    ppermute x1, starting transfers between devices, body(): recv_b = lax.ppermute(recv_a, 'core', SWAP)  4.88 us
    pallas_call x1, Pallas kernels, degrees(): pl.pallas_call(degree_kernel, grid_spec=pltpu.PrefetchScalarGridSpec(num_...  4.19 us
    unnamed x14, local copies, waits for them, and re-layouts  2.54 us
  transfers between devices with their start and end apart: 1, of which 1 were waited for; matrix products, arithmetic and copies ran while one was open for 0% of the time, Pallas kernels for 0%

profile of v2, /device:TPU:1, one launch (start us, length us, event | category | flops | bytes accessed | tf_op | source)
XLA Modules:
  0.0 98.7 jit_solution(4220559187115096027)
XLA Ops:
  0.6 0.0 copy-start
  1.4 0.0 copy-start.3
  1.4 0.9 copy-done.3
  2.3 0.0 copy-start.4
  2.3 1.0 copy-done.4
  3.3 0.7 copy-done.5
  4.0 4.2 %degrees.1 = (bf16[16,160,128]{2,1,0:T(8,128)(2,1)S(1)}, s32[1,256]{1,0:T(1,128)S(1)}) custom-call(s32[1,1]{1,0:T(1,128)S(6)} %copy.27.count, s32[256]{0:T(256)S(1)} %copy-done.5, s32[2,256]{1,0:T(2,128)S(1)} %bitcast.14, bf16[128,128]{1,0:T(8,128)(2,1)S(1)} %copy-done.3, bf16[256,128,128]{2,1,0:T(8,128)(2,1)} %bitcast.12), custom_call_target="tpu_custom_call" | custom-call | tf_op jit(solution)/shard_map/degrees/pallas_call | solution.py:76
  8.2 25.6 %all_to_all.25.recv_a = bf16[16,160,128]{2,1,0:T(8,128)(2,1)S(1)} all-to-all(bf16[16,160,128]{2,1,0:T(8,128)(2,1)S(1)} %get-tuple-element.8), channel_id=1, replica_groups=mesh['z'=8,'y_lo'=2,'core'=2,'y_hi'=2,'x'=4] {'z','y_lo'}, dimensions={0} | all-to-all | bytes 1310720 | tf_op jit(solution)/shard_map/all_to_all | solution.py:192
  33.8 4.9 %collective-permute-start = (bf16[16,160,128]{2,1,0:T(8,128)(2,1)S(1)}, bf16[16,160,128]{2,1,0:T(8,128)(2,1)S(1)}, u32[]{:S(2)}, u32[]{:S(2)}) collective-permute-start(bf16[16,160,128]{2,1,0:T(8,128)(2,1)S(1)} %all_to_all.25.recv_a), channel_id=1, source_target_pairs={{0,8},{8,0},{1,9},{9,1},{2,10},{10,2},{3,11},{11,3},{4,12},{12,4},... | collective-permute-start | bytes 1966088 | tf_op jit(solution)/shard_map/ppermute | solution.py:193
  38.7 1.7 %collective-permute-done.recv_b = bf16[16,160,128]{2,1,0:T(8,128)(2,1)S(1)} collective-permute-done((bf16[16,160,128]{2,1,0:T(8,128)(2,1)S(1)}, bf16[16,160,128]{2,1,0:T(8,128)(2,1)S(1)}, u32[]{:S(2)}, u32[]{:S(2)}) %collective-permute-start) | collective-permute-done | bytes 655392 | tf_op jit(solution)/shard_map/ppermute | solution.py:193
  40.4 0.0 copy-done
  40.4 5.1 %product.1 = bf16[8,144,128]{2,1,0:T(8,128)(2,1)S(1)} custom-call(s32[1,256]{1,0:T(1,128)S(1)} %get-tuple-element.7.slots, bf16[16,160,128]{2,1,0:T(8,128)(2,1)S(1)} %all_to_all.25.recv_a, bf16[16,160,128]{2,1,0:T(8,128)(2,1)S(1)} %collective-permute-done.recv_b, bf16[256,128,128]{2,1,0:T(8,128)(2,1)S(1)} %bitcast.13), custom_call_target="tpu_custom_call" | custom-call | tf_op jit(solution)/shard_map/product/pallas_call | solution.py:138
  45.5 17.0 %all_to_all.26.parts = bf16[8,144,128]{2,1,0:T(8,128)(2,1)S(1)} all-to-all(bf16[8,144,128]{2,1,0:T(8,128)(2,1)S(1)} %product.1), channel_id=1, replica_groups=mesh['z'=8,'y_lo'=2,'core'=2,'y_hi'=2,'x'=4] {'y_hi','x'}, dimensions={0} | all-to-all | bytes 589824 | tf_op jit(solution)/shard_map/all_to_all | solution.py:196
  62.5 0.0 copy-done.1
  62.5 0.0 copy-done.2
  62.5 0.0 copy-done.6
  62.5 0.9 nodes.1
  63.4 11.6 %all_to_all.27 = f32[32,9,1,128]{3,2,1,0:T(1,128)S(1)} all-to-all(f32[32,9,1,128]{3,2,1,0:T(1,128)S(1)} %get-tuple-element.10), channel_id=1, replica_groups=mesh['z'=8,'y_lo'=2,'core'=2,'y_hi'=2,'x'=4] {'y_lo','core','y_hi','x'}, dimensions={0} | all-to-all | bytes 294912 | tf_op jit(solution)/shard_map/all_to_all | solution.py:198
  75.0 0.1 reduce_sum.18
  75.2 9.4 %all_to_all.28 = f32[8,9,1,128]{3,2,1,0:T(1,128)S(1)} all-to-all(f32[8,9,1,128]{3,2,1,0:T(1,128)S(1)} %broadcast_in_dim.7), channel_id=1, replica_groups=mesh['z'=8,'y_lo'=2,'core'=2,'y_hi'=2,'x'=4] {'z'}, dimensions={0} | all-to-all | bytes 73728 | tf_op jit(solution)/shard_map/all_to_all | solution.py:185
  84.6 0.1 broadcast_in_dim.8
  84.7 12.7 %all_to_all.29 = f32[32,9,1,128]{3,2,1,0:T(1,128)S(1)} all-to-all(f32[32,9,1,128]{3,2,1,0:T(1,128)S(1)} %broadcast_in_dim.8), channel_id=1, replica_groups=mesh['z'=8,'y_lo'=2,'core'=2,'y_hi'=2,'x'=4] {'y_lo','core','y_hi','x'}, dimensions={0} | all-to-all | bytes 294912 | tf_op jit(solution)/shard_map/all_to_all | solution.py:185
  97.4 0.6 slice_bitcast_fusion
  98.0 0.7 pad_maximum_fusion
  (10 shorter events, 0.1 us)
Async XLA Ops:
  0.6 39.8 %copy-start = (bf16[1,1,256,128,128]{4,3,2,1,0:T(8,128)(2,1)S(1)}, bf16[1,1,256,128,128]{4,3,2,1,0:T(8,128)(2,1)}, u32[]{:S(2)}) copy-start(bf16[1,1,256,128,128]{4,3,2,1,0:T(8,128)(2,1)} %param.12) | copy-start | bytes 25165828
  1.4 0.9 copy-start.3
  2.3 1.0 copy-start.4
  3.3 0.7 copy-start.5
  4.0 58.5 %copy-start.1 = (bf16[128,256]{1,0:T(8,128)(2,1)S(1)}, bf16[128,256]{1,0:T(8,128)(2,1)}, u32[]{:S(2)}) copy-start(bf16[128,256]{1,0:T(8,128)(2,1)} %weight.1) | copy-start | bytes 196612
  4.0 58.5 %copy-start.2 = (bf16[128,256]{1,0:T(8,128)(2,1)S(1)}, bf16[128,256]{1,0:T(8,128)(2,1)}, u32[]{:S(2)}) copy-start(bf16[128,256]{1,0:T(8,128)(2,1)} %cotangent.1) | copy-start | bytes 196612
  4.0 58.5 %copy-start.6 = (f32[256]{0:T(256)S(1)}, f32[256]{0:T(256)}, u32[]{:S(2)}) copy-start(f32[256]{0:T(256)} %param.10) | copy-start | bytes 3076
  33.8 6.6 %collective-permute-start = (bf16[16,160,128]{2,1,0:T(8,128)(2,1)S(1)}, bf16[16,160,128]{2,1,0:T(8,128)(2,1)S(1)}, u32[]{:S(2)}, u32[]{:S(2)}) collective-permute-start(bf16[16,160,128]{2,1,0:T(8,128)(2,1)S(1)} %all_to_all.25.recv_a), channel_id=1, source_target_pairs={{0,8},{8,0},{1,9},{9,1},{2,10},{10,2},{3,11},{11,3},{4,12},{12,4},... | collective-permute-start | bytes 1966088 | tf_op jit(solution)/shard_map/ppermute | solution.py:193

commit v3 on v2

v3 whole, which is shorter than its diff:
```python
import functools

import jax
import jax.numpy as jnp
from jax import lax
from jax.experimental import pallas as pl
from jax.experimental.pallas import tpu as pltpu
from jax.sharding import Mesh, PartitionSpec as P

ROW = ("z", "y_lo", "core")
COL = ("y_hi", "x")
SAME_CORE_ROW = ("z", "y_lo")
PLANE = ("y_lo", "core", "y_hi", "x")
SWAP = [(0, 1), (1, 0)]
CHUNK = 32
F32 = jnp.float32
BF16 = jnp.bfloat16


def degree_kernel(count, perm, pos_hbm, feats_hbm, tiles_hbm, send_ref, slot_ref, tiles, pos, feats, sums, sem, small):
    steps = 256 // CHUNK

    def chunk_copy(step):
        part = pl.ds(step * CHUNK, CHUNK)
        return pltpu.make_async_copy(tiles_hbm.at[part], tiles.at[part], sem.at[step])

    pos_copy = pltpu.make_async_copy(pos_hbm, pos, small.at[0])
    feats_copy = pltpu.make_async_copy(feats_hbm, feats, small.at[1])
    pos_copy.start()
    for step in range(steps):
        chunk_copy(step).start()
    feats_copy.start()
    live_count = count[0, 0]
    row, col, core = lax.axis_index(ROW), lax.axis_index(COL), lax.axis_index("core")
    pos_copy.wait()
    own_row = jnp.zeros((1, 256), jnp.int32)
    own_col = jnp.zeros((1, 256), jnp.int32)
    for v in range(8):
        own_row += jnp.where(pos[0:1, :] == v, perm[row * 8 + v] - row * 8, 0)
    for v in range(32):
        own_col += jnp.where(pos[1:2, :] == v, perm[col * 32 + v] - col * 32, 0)
    place = (own_col >> 1) + 16 * ((own_col & 1) ^ core)
    slot = lax.broadcasted_iota(jnp.int32, (1, 256), 1)
    place = jnp.where(slot < live_count, place, 512)
    dense = own_row * 32 + place
    match = lax.broadcasted_iota(jnp.int32, (256, 256), 0) == dense
    number = lax.broadcasted_iota(jnp.int32, (16, 256), 1) + 1
    found = lax.dot_general(
        number.astype(F32).astype(BF16),
        match.astype(F32).astype(BF16),
        (((1,), (1,)), ((), ())),
        preferred_element_type=F32,
    )
    slot_ref[...] = found[0:1, :].astype(jnp.int32) - 1

    @pl.loop(0, steps)
    def _(step):
        chunk_copy(step).wait()
        base = step * CHUNK

        @pl.when(base < live_count)
        def _():
            for group in range(CHUNK // 8):
                rows = []
                for u in range(8):
                    tile = tiles[base + group * 8 + u].astype(F32)
                    rows.append(jnp.sum(tile, axis=0, keepdims=True))
                sums[pl.ds(base + group * 8, 8), :] = jnp.concatenate(rows, axis=0)

        @pl.when(base >= live_count)
        def _():
            sums[pl.ds(base, CHUNK), :] = jnp.zeros((CHUNK, 128), F32)

    pick = (lax.broadcasted_iota(jnp.int32, (32, 256), 0) == place).astype(F32)
    col_part = jnp.dot(
        pick, sums[...], precision=lax.Precision.HIGHEST, preferred_element_type=F32
    ).astype(BF16)
    feats_copy.wait()
    for m in range(16):
        send_ref[m, 0:128, :] = feats[...]
        send_ref[m, 128:160, :] = col_part


def degrees(count, perm, pos, features, packed):
    smem = pl.BlockSpec(memory_space=pltpu.SMEM)
    vmem = pl.BlockSpec(memory_space=pltpu.VMEM)
    hbm = pl.BlockSpec(memory_space=pltpu.HBM)
    return pl.pallas_call(
        degree_kernel,
        in_specs=[smem, smem, hbm, hbm, hbm],
        out_specs=[vmem, vmem, vmem],
        scratch_shapes=[
            pltpu.VMEM((2, 256), jnp.int32),
            pltpu.VMEM((128, 128), BF16),
            pltpu.VMEM((256, 128), F32),
            pltpu.SemaphoreType.DMA((256 // CHUNK,)),
            pltpu.SemaphoreType.DMA((2,)),
        ],
        out_shape=[
            jax.ShapeDtypeStruct((16, 160, 128), BF16),
            jax.ShapeDtypeStruct((1, 256), jnp.int32),
            pltpu.VMEM((256, 128, 128), BF16),
        ],
        compiler_params=pltpu.CompilerParams(vmem_limit_bytes=16 << 20),
        name="degrees",
    )(count, perm, pos, features, packed)


def arrange_kernel(slots, tiles, dense, sums_ref):
    @pl.loop(0, 8)
    def _(i):
        total = jnp.zeros((128, 128), F32)
        for place in range(32):
            slot = slots[0, i * 32 + place]
            tile = jnp.where(slot >= 0, tiles[jnp.maximum(slot, 0)], jnp.zeros((), BF16))
            rows = pl.ds(pl.multiple_of(i * 128, 128), 128)
            lane = place % 8 * 128
            dense[place // 8, rows, lane : lane + 128] = tile
            total += tile.astype(F32)
        sums = jnp.broadcast_to(jnp.sum(total.T, axis=0, keepdims=True), (8, 128))
        high = sums.astype(BF16)
        low = (sums - high.astype(F32)).astype(BF16)
        sums_ref[i] = jnp.concatenate([high, low], axis=0)


def arrange(slots, tiles):
    vmem = pl.BlockSpec(memory_space=pltpu.VMEM)
    return pl.pallas_call(
        arrange_kernel,
        in_specs=[pl.BlockSpec(memory_space=pltpu.SMEM), vmem],
        out_specs=[vmem, vmem],
        out_shape=[
            pltpu.VMEM((4, 1024, 1024), BF16),
            pltpu.VMEM((8, 16, 128), BF16),
        ],
        cost_estimate=pl.CostEstimate(flops=0, bytes_accessed=16 << 20, transcendentals=0),
        compiler_params=pltpu.CompilerParams(vmem_limit_bytes=16 << 20),
        name="arrange",
    )(slots, tiles)


def product_kernel(recv_a, recv_b, dense, sums, out, rhs, acc):
    from_a = jnp.sum(recv_a[:, 128:160, :].astype(F32), axis=0)
    from_b = jnp.sum(recv_b[:, 128:160, :].astype(F32), axis=0)
    degree = 1.0 + from_a + jnp.concatenate([from_b[16:32], from_b[0:16]], axis=0)
    scale = jnp.concatenate([lax.rsqrt(degree), jnp.zeros((96, 128), F32)], axis=0).T
    for part in range(4):
        for b in range(part * 8, part * 8 + 8):
            feat = recv_a[b, 0:128, :] if b < 16 else recv_b[b - 16, 0:128, :]
            scaled = scale[:, b : b + 1] * feat.astype(F32)
            rhs[b * 128 : b * 128 + 128, :] = scaled.astype(BF16)
        term = jnp.dot(
            dense[part], rhs[part * 1024 : part * 1024 + 1024, :], preferred_element_type=F32
        )
        if part == 0:
            acc[...] = term
        elif part < 3:
            acc[...] += term
        else:
            total = (acc[...] + term).astype(BF16)
    for i in range(8):
        out[i, 0:128, :] = total[i * 128 : i * 128 + 128, :]
        out[i, 128:144, :] = sums[i]


def product(recv_a, recv_b, dense, sums):
    vmem = pl.BlockSpec(memory_space=pltpu.VMEM)
    return pl.pallas_call(
        product_kernel,
        in_specs=[vmem, vmem, vmem, vmem],
        out_specs=vmem,
        scratch_shapes=[pltpu.VMEM((4096, 128), BF16), pltpu.VMEM((1024, 128), F32)],
        out_shape=jax.ShapeDtypeStruct((8, 144, 128), BF16),
        compiler_params=pltpu.CompilerParams(vmem_limit_bytes=24 << 20),
        name="product",
    )(recv_a, recv_b, dense, sums)


def node_kernel(parts, weight, bias, cotangent, hidden_ref, terms_ref):
    total = jnp.sum(parts[...].astype(F32), axis=0)
    row_degree = jnp.broadcast_to(1.0 + total[128:129, :] + total[136:137, :], (128, 128)).T
    aggregated = (lax.rsqrt(row_degree) * total[0:128, :]).astype(BF16)
    preact = jnp.dot(aggregated, weight[...], preferred_element_type=F32) + bias[...]
    logistic = jax.nn.sigmoid(preact)
    hidden_ref[...] = (preact * logistic).astype(BF16)
    grad = (
        cotangent[...].astype(F32) * logistic * (1.0 + preact * (1.0 - logistic))
    ).astype(BF16)
    weight_part = lax.dot_general(
        aggregated, grad, (((0,), (0,)), ((), ())), preferred_element_type=F32
    )
    bias_part = jnp.sum(grad.astype(F32), axis=0, keepdims=True)
    for k in range(32):
        half, f = k // 16, (k % 16) * 8
        for s in range(8):
            terms_ref[k, s, :, :] = weight_part[f + s : f + s + 1, half * 128 : half * 128 + 128]
        terms_ref[k, 8, :, :] = (
            bias_part[:, k * 128 : k * 128 + 128] if k < 2 else jnp.zeros((1, 128), F32)
        )


def nodes(parts, weight, bias, cotangent):
    return pl.pallas_call(
        node_kernel,
        out_shape=[
            jax.ShapeDtypeStruct((128, 256), BF16),
            jax.ShapeDtypeStruct((32, 9, 1, 128), F32),
        ],
        compiler_params=pltpu.CompilerParams(vmem_limit_bytes=16 << 20),
        name="nodes",
    )(parts, weight, bias, cotangent)


def finish_kernel(every, weight_ref, bias_ref):
    for k in range(32):
        half, f = k // 16, (k % 16) * 8
        for s in range(8):
            weight_ref[f + s : f + s + 1, half * 128 : half * 128 + 128] = every[k, s, :, :]
    for k in range(2):
        bias_ref[:, k * 128 : k * 128 + 128] = every[k, 8, :, :]


def finish(every):
    return pl.pallas_call(
        finish_kernel,
        out_shape=[
            jax.ShapeDtypeStruct((128, 256), F32),
            jax.ShapeDtypeStruct((1, 256), F32),
        ],
        compiler_params=pltpu.CompilerParams(vmem_limit_bytes=16 << 20),
        name="finish",
    )(every)


def gather(x, axes, count):
    return lax.all_to_all(jnp.broadcast_to(x[None], (count,) + x.shape), axes, 0, 0)


def body(features, weight, bias, cotangent, tile_values, tile_pos, tile_count, block_perm):
    packed = tile_values[0, 0]
    in_hbm = [
        pltpu.with_memory_space_constraint(x, pltpu.HBM)
        for x in (block_perm, tile_pos[0, 0], features, packed)
    ]
    send, slots, held = degrees(tile_count, *in_hbm)
    recv_a = lax.all_to_all(send, SAME_CORE_ROW, 0, 0)
    recv_b = lax.ppermute(recv_a, "core", SWAP)
    partial = product(recv_a, recv_b, *arrange(slots, held))
    received = lax.all_to_all(partial, COL, 0, 0)
    hidden, terms = nodes(received, weight, bias[None], cotangent)
    own_terms = jnp.sum(lax.all_to_all(terms, PLANE, 0, 0), axis=0)
    total = jnp.sum(gather(own_terms, ("z",), 8), axis=0) * lax.rsqrt(F32(32768.0))
    weight_grad, bias_grad = finish(gather(total, PLANE, 32))
    return hidden, weight_grad, bias_grad[0]


def solution(mesh):
    split = Mesh(mesh.devices.reshape(8, 2, 2, 2, 4), ("z", "y_lo", "core", "y_hi", "x"))
    placed = (
        P(COL + ROW, None),
        P(),
        P(),
        P(ROW + COL, None),
        P(ROW, COL, None, None, None),
        P(ROW, COL, None, None),
        P(ROW, COL),
        P(),
    )
    return jax.shard_map(
        body,
        mesh=split,
        in_specs=placed,
        out_specs=(P(ROW + COL, None), P(), P()),
        check_vma=False,
    )
```

time: 99.1 us -> 95.7 us (0.966)
  local copies, waits for them, and re-layouts: 3.27 us -> 0.11 us
  blocking collectives: 76.3 us -> 79 us
  starting transfers between devices: 4.88 us -> 2.18 us
  Pallas kernels: 10.2 us -> 12.8 us
  waiting for transfers between devices: 1.72 us -> 0.01 us
    all_to_all x1, blocking collectives: 25.6 us -> 29.5 us  [body(): recv_a = lax.all_to_all(send, SAME_CORE_ROW, 0, 0)]
    ppermute x1, starting transfers between devices: 4.88 us -> 2.18 us  [body(): recv_b = lax.ppermute(recv_a, 'core', SWAP)]
    pallas_call x2 -> x4, Pallas kernels: 9.32 us -> 11.9 us  [the longest x1 4.48 us: degrees(): pl.pallas_call(degree_kernel, in_specs=[smem, smem, hbm, hbm, hbm], out_s...]
    unnamed x14 -> x6, local copies, waits for them, and re-layouts: 2.54 us -> 0.01 us
    ppermute x1, waiting for transfers between devices: 1.72 us -> 0.01 us  [body(): recv_b = lax.ppermute(recv_a, 'core', SWAP)]
    all_to_all x1, blocking collectives: 17 us -> 15.7 us  [body(): received = lax.all_to_all(partial, COL, 0, 0)]
  transfers between devices with their start and end apart: 1 -> 1, of which waited for: 1 -> 0; matrix products, arithmetic and copies ran while one was open for 0% -> 0% of each run, Pallas kernels for 0% -> 4%
where the time goes in v3:
time: 95.7 us; the launch traced here: 95.5 us
  blocking collectives  79 us (83%)
  Pallas kernels  12.8 us (13%)
  starting transfers between devices  2.18 us (2%)
  between operations  1.34 us (1%)
    all_to_all x1, blocking collectives, body(): recv_a = lax.all_to_all(send, SAME_CORE_ROW, 0, 0)  29.5 us
    all_to_all x2, blocking collectives, gather(): lax.all_to_all(jnp.broadcast_to(x[None], (count,) + x.shape), axes, 0, 0)  22.1 us
    all_to_all x1, blocking collectives, body(): received = lax.all_to_all(partial, COL, 0, 0)  15.7 us
    all_to_all x1, blocking collectives, body(): own_terms = jnp.sum(lax.all_to_all(terms, PLANE, 0, 0), axis=0)  11.6 us
    pallas_call x1, Pallas kernels, degrees(): pl.pallas_call(degree_kernel, in_specs=[smem, smem, hbm, hbm, hbm], out_s...  4.48 us
    pallas_call x1, Pallas kernels, arrange(): pl.pallas_call(arrange_kernel, in_specs=[pl.BlockSpec(memory_space=pltpu....  4.06 us
    pallas_call x1, Pallas kernels, product(): pl.pallas_call(product_kernel, in_specs=[vmem, vmem, vmem, vmem], out_spe...  2.65 us
    ppermute x1, starting transfers between devices, body(): recv_b = lax.ppermute(recv_a, 'core', SWAP)  2.18 us
  transfers between devices with their start and end apart: 1, of which 0 were waited for; matrix products, arithmetic and copies ran while one was open for 0% of the time, Pallas kernels for 4%

profile of v3, /device:TPU:1, one launch (start us, length us, event | category | flops | bytes accessed | tf_op | source)
XLA Modules:
  0.0 95.5 jit_solution(9362529985376898118)
XLA Ops:
  1.3 4.5 %degrees.1 = (bf16[16,160,128]{2,1,0:T(8,128)(2,1)S(1)}, s32[1,256]{1,0:T(1,128)S(1)}, bf16[256,128,128]{2,1,0:T(8,128)(2,1)S(1)}) custom-call(s32[1,1]{1,0:T(1,128)S(6)} %copy.13.count, s32[256]{0:T(256)} %perm.1, s32[2,256]{1,0:T(2,128)} %bitcast.6, bf16[128,128]{1,0:T(8,128)(2,1)} %feats_hbm.1, bf16[256,128,128]{2,1,0:T(8,128)(2,1)} %bitcast.5), custom_call_target="tpu_custom_call" | custom-call | tf_op jit(solution)/shard_map/degrees/pallas_call | solution.py:88
  5.8 29.5 %all_to_all.25.recv_a = bf16[16,160,128]{2,1,0:T(8,128)(2,1)S(1)} all-to-all(bf16[16,160,128]{2,1,0:T(8,128)(2,1)S(1)} %get-tuple-element.12), channel_id=1, replica_groups=mesh['z'=8,'y_lo'=2,'core'=2,'y_hi'=2,'x'=4] {'z','y_lo'}, dimensions={0} | all-to-all | bytes 1310720 | tf_op jit(solution)/shard_map/all_to_all | solution.py:246
  35.3 2.2 %collective-permute-start = (bf16[16,160,128]{2,1,0:T(8,128)(2,1)S(1)}, bf16[16,160,128]{2,1,0:T(8,128)(2,1)S(1)}, u32[]{:S(2)}, u32[]{:S(2)}) collective-permute-start(bf16[16,160,128]{2,1,0:T(8,128)(2,1)S(1)} %all_to_all.25.recv_a), channel_id=1, source_target_pairs={{0,8},{8,0},{1,9},{9,1},{2,10},{10,2},{3,11},{11,3},{4,12},{12,4},... | collective-permute-start | bytes 1966088 | tf_op jit(solution)/shard_map/ppermute | solution.py:247
  37.5 0.0 copy-start
  37.5 0.0 copy-start.1
  37.5 0.0 copy-start.2
  37.5 4.1 %arrange.1 = (bf16[4,1024,1024]{2,1,0:T(8,128)(2,1)S(1)}, bf16[8,16,128]{2,1,0:T(8,128)(2,1)S(1)}) custom-call(s32[1,256]{1,0:T(1,128)S(1)} %get-tuple-element.13.slots, bf16[256,128,128]{2,1,0:T(8,128)(2,1)S(1)} %get-tuple-element.14.tiles), custom_call_target="tpu_custom_call" | custom-call | bytes 16777216 | tf_op jit(solution)/shard_map/arrange/pallas_call | solution.py:128
  41.6 0.0 collective-permute-done.recv_b
  41.6 2.7 %product.1 = bf16[8,144,128]{2,1,0:T(8,128)(2,1)S(1)} custom-call(bf16[16,160,128]{2,1,0:T(8,128)(2,1)S(1)} %all_to_all.25.recv_a, bf16[16,160,128]{2,1,0:T(8,128)(2,1)S(1)} %collective-permute-done.recv_b, bf16[4,1024,1024]{2,1,0:T(8,128)(2,1)S(1)} %get-tuple-element.15.dense, bf16[8,16,128]{2,1,0:T(8,128)(2,1)S(1)} %get-tuple-element.16.sums), custom_call_target="tpu_custom_call" | custom-call | tf_op jit(solution)/shard_map/product/pallas_call | solution.py:168
  44.2 15.7 %all_to_all.26.parts = bf16[8,144,128]{2,1,0:T(8,128)(2,1)S(1)} all-to-all(bf16[8,144,128]{2,1,0:T(8,128)(2,1)S(1)} %product.1), channel_id=1, replica_groups=mesh['z'=8,'y_lo'=2,'core'=2,'y_hi'=2,'x'=4] {'y_hi','x'}, dimensions={0} | all-to-all | bytes 589824 | tf_op jit(solution)/shard_map/all_to_all | solution.py:249
  60.0 0.0 copy-done
  60.0 0.0 copy-done.1
  60.0 0.0 copy-done.2
  60.0 0.9 nodes.1
  60.9 11.6 %all_to_all.27 = f32[32,9,1,128]{3,2,1,0:T(1,128)S(1)} all-to-all(f32[32,9,1,128]{3,2,1,0:T(1,128)S(1)} %get-tuple-element.18), channel_id=1, replica_groups=mesh['z'=8,'y_lo'=2,'core'=2,'y_hi'=2,'x'=4] {'y_lo','core','y_hi','x'}, dimensions={0} | all-to-all | bytes 294912 | tf_op jit(solution)/shard_map/all_to_all | solution.py:251
  72.5 0.1 reduce_sum.18
  72.6 9.4 %all_to_all.28 = f32[8,9,1,128]{3,2,1,0:T(1,128)S(1)} all-to-all(f32[8,9,1,128]{3,2,1,0:T(1,128)S(1)} %broadcast_in_dim.7), channel_id=1, replica_groups=mesh['z'=8,'y_lo'=2,'core'=2,'y_hi'=2,'x'=4] {'z'}, dimensions={0} | all-to-all | bytes 73728 | tf_op jit(solution)/shard_map/all_to_all | solution.py:236
  82.1 0.1 broadcast_in_dim.8
  82.1 12.7 %all_to_all.29.every = f32[32,9,1,128]{3,2,1,0:T(1,128)S(1)} all-to-all(f32[32,9,1,128]{3,2,1,0:T(1,128)S(1)} %broadcast_in_dim.8), channel_id=1, replica_groups=mesh['z'=8,'y_lo'=2,'core'=2,'y_hi'=2,'x'=4] {'y_lo','core','y_hi','x'}, dimensions={0} | all-to-all | bytes 294912 | tf_op jit(solution)/shard_map/all_to_all | solution.py:236
  94.8 0.7 finish.1
  (3 shorter events, 0.1 us)
Async XLA Ops:
  35.3 6.3 %collective-permute-start = (bf16[16,160,128]{2,1,0:T(8,128)(2,1)S(1)}, bf16[16,160,128]{2,1,0:T(8,128)(2,1)S(1)}, u32[]{:S(2)}, u32[]{:S(2)}) collective-permute-start(bf16[16,160,128]{2,1,0:T(8,128)(2,1)S(1)} %all_to_all.25.recv_a), channel_id=1, source_target_pairs={{0,8},{8,0},{1,9},{9,1},{2,10},{10,2},{3,11},{11,3},{4,12},{12,4},... | collective-permute-start | bytes 1966088 | tf_op jit(solution)/shard_map/ppermute | solution.py:247
  37.5 22.5 %copy-start = (bf16[128,256]{1,0:T(8,128)(2,1)S(1)}, bf16[128,256]{1,0:T(8,128)(2,1)}, u32[]{:S(2)}) copy-start(bf16[128,256]{1,0:T(8,128)(2,1)} %weight.1) | copy-start | bytes 196612
  37.5 22.5 %copy-start.1 = (bf16[128,256]{1,0:T(8,128)(2,1)S(1)}, bf16[128,256]{1,0:T(8,128)(2,1)}, u32[]{:S(2)}) copy-start(bf16[128,256]{1,0:T(8,128)(2,1)} %cotangent.1) | copy-start | bytes 196612
  37.5 22.5 %copy-start.2 = (f32[256]{0:T(256)S(1)}, f32[256]{0:T(256)}, u32[]{:S(2)}) copy-start(f32[256]{0:T(256)} %param.10) | copy-start | bytes 3076

commit v4 on v3

--- a/solution.py
+++ b/solution.py
@@ -12,7 +12,7 @@
 SAME_CORE_ROW = ("z", "y_lo")
 PLANE = ("y_lo", "core", "y_hi", "x")
 SWAP = [(0, 1), (1, 0)]
-CHUNK = 32
+CHUNK = 16
 F32 = jnp.float32
 BF16 = jnp.bfloat16
 
@@ -27,10 +27,14 @@
     pos_copy = pltpu.make_async_copy(pos_hbm, pos, small.at[0])
     feats_copy = pltpu.make_async_copy(feats_hbm, feats, small.at[1])
     pos_copy.start()
+    live_count = count[0, 0]
     for step in range(steps):
-        chunk_copy(step).start()
+
+        @pl.when(step * CHUNK < live_count)
+        def _():
+            chunk_copy(step).start()
+
     feats_copy.start()
-    live_count = count[0, 0]
     row, col, core = lax.axis_index(ROW), lax.axis_index(COL), lax.axis_index("core")
     pos_copy.wait()
     own_row = jnp.zeros((1, 256), jnp.int32)
@@ -51,15 +55,17 @@
         (((1,), (1,)), ((), ())),
         preferred_element_type=F32,
     )
-    slot_ref[...] = found[0:1, :].astype(jnp.int32) - 1
+    found = found[0:1, :].astype(jnp.int32)
+    slot_ref[...] = jnp.where(found == 0, 256, found - 1)
+    tiles[256] = jnp.zeros((128, 128), BF16)
 
     @pl.loop(0, steps)
     def _(step):
-        chunk_copy(step).wait()
         base = step * CHUNK
 
         @pl.when(base < live_count)
         def _():
+            chunk_copy(step).wait()
             for group in range(CHUNK // 8):
                 rows = []
                 for u in range(8):
@@ -71,14 +77,15 @@
         def _():
             sums[pl.ds(base, CHUNK), :] = jnp.zeros((CHUNK, 128), F32)
 
-    pick = (lax.broadcasted_iota(jnp.int32, (32, 256), 0) == place).astype(F32)
-    col_part = jnp.dot(
-        pick, sums[...], precision=lax.Precision.HIGHEST, preferred_element_type=F32
-    ).astype(BF16)
+    pick = (lax.broadcasted_iota(jnp.int32, (32, 256), 0) == place).astype(F32).astype(BF16)
+    high = sums[...].astype(BF16)
+    low = (sums[...] - high.astype(F32)).astype(BF16)
+    col_part = jnp.dot(pick, high, preferred_element_type=F32)
+    col_part += jnp.dot(pick, low, preferred_element_type=F32)
     feats_copy.wait()
     for m in range(16):
         send_ref[m, 0:128, :] = feats[...]
-        send_ref[m, 128:160, :] = col_part
+        send_ref[m, 128:160, :] = col_part.astype(BF16)
 
 
 def degrees(count, perm, pos, features, packed):
@@ -99,47 +106,39 @@
         out_shape=[
             jax.ShapeDtypeStruct((16, 160, 128), BF16),
             jax.ShapeDtypeStruct((1, 256), jnp.int32),
-            pltpu.VMEM((256, 128, 128), BF16),
+            pltpu.VMEM((257, 128, 128), BF16),
         ],
         compiler_params=pltpu.CompilerParams(vmem_limit_bytes=16 << 20),
         name="degrees",
     )(count, perm, pos, features, packed)
 
 
-def arrange_kernel(slots, tiles, dense, sums_ref):
+def row_sum_kernel(slots, tiles, sums_ref):
     @pl.loop(0, 8)
     def _(i):
         total = jnp.zeros((128, 128), F32)
         for place in range(32):
-            slot = slots[0, i * 32 + place]
-            tile = jnp.where(slot >= 0, tiles[jnp.maximum(slot, 0)], jnp.zeros((), BF16))
-            rows = pl.ds(pl.multiple_of(i * 128, 128), 128)
-            lane = place % 8 * 128
-            dense[place // 8, rows, lane : lane + 128] = tile
-            total += tile.astype(F32)
+            total += tiles[slots[0, i * 32 + place]].astype(F32)
         sums = jnp.broadcast_to(jnp.sum(total.T, axis=0, keepdims=True), (8, 128))
         high = sums.astype(BF16)
         low = (sums - high.astype(F32)).astype(BF16)
         sums_ref[i] = jnp.concatenate([high, low], axis=0)
 
 
-def arrange(slots, tiles):
+def row_sums(slots, tiles):
     vmem = pl.BlockSpec(memory_space=pltpu.VMEM)
     return pl.pallas_call(
-        arrange_kernel,
+        row_sum_kernel,
         in_specs=[pl.BlockSpec(memory_space=pltpu.SMEM), vmem],
-        out_specs=[vmem, vmem],
-        out_shape=[
-            pltpu.VMEM((4, 1024, 1024), BF16),
-            pltpu.VMEM((8, 16, 128), BF16),
-        ],
-        cost_estimate=pl.CostEstimate(flops=0, bytes_accessed=16 << 20, transcendentals=0),
-        compiler_params=pltpu.CompilerParams(vmem_limit_bytes=16 << 20),
-        name="arrange",
+        out_specs=vmem,
+        out_shape=pltpu.VMEM((8, 16, 128), BF16),
+        cost_estimate=pl.CostEstimate(flops=0, bytes_accessed=6 << 20, transcendentals=0),
+        compiler_params=pltpu.CompilerParams(vmem_limit_bytes=16 << 20),
+        name="row_sums",
     )(slots, tiles)
 
 
-def product_kernel(recv_a, recv_b, dense, sums, out, rhs, acc):
+def product_kernel(slots, recv_a, recv_b, tiles, sums, out, rhs, acc):
     from_a = jnp.sum(recv_a[:, 128:160, :].astype(F32), axis=0)
     from_b = jnp.sum(recv_b[:, 128:160, :].astype(F32), axis=0)
     degree = 1.0 + from_a + jnp.concatenate([from_b[16:32], from_b[0:16]], axis=0)
@@ -149,8 +148,17 @@
             feat = recv_a[b, 0:128, :] if b < 16 else recv_b[b - 16, 0:128, :]
             scaled = scale[:, b : b + 1] * feat.astype(F32)
             rhs[b * 128 : b * 128 + 128, :] = scaled.astype(BF16)
+        dense = jnp.concatenate(
+            [
+                jnp.concatenate(
+                    [tiles[slots[0, i * 32 + part * 8 + q]] for q in range(8)], axis=1
+                )
+                for i in range(8)
+            ],
+            axis=0,
+        )
         term = jnp.dot(
-            dense[part], rhs[part * 1024 : part * 1024 + 1024, :], preferred_element_type=F32
+            dense, rhs[part * 1024 : part * 1024 + 1024, :], preferred_element_type=F32
         )
         if part == 0:
             acc[...] = term
@@ -163,17 +171,17 @@
         out[i, 128:144, :] = sums[i]
 
 
-def product(recv_a, recv_b, dense, sums):
+def product(slots, recv_a, recv_b, tiles, sums):
     vmem = pl.BlockSpec(memory_space=pltpu.VMEM)
     return pl.pallas_call(
         product_kernel,
-        in_specs=[vmem, vmem, vmem, vmem],
+        in_specs=[pl.BlockSpec(memory_space=pltpu.SMEM), vmem, vmem, vmem, vmem],
         out_specs=vmem,
         scratch_shapes=[pltpu.VMEM((4096, 128), BF16), pltpu.VMEM((1024, 128), F32)],
         out_shape=jax.ShapeDtypeStruct((8, 144, 128), BF16),
         compiler_params=pltpu.CompilerParams(vmem_limit_bytes=24 << 20),
         name="product",
-    )(recv_a, recv_b, dense, sums)
+    )(slots, recv_a, recv_b, tiles, sums)
 
 
 def node_kernel(parts, weight, bias, cotangent, hidden_ref, terms_ref):
@@ -245,7 +253,7 @@
     send, slots, held = degrees(tile_count, *in_hbm)
     recv_a = lax.all_to_all(send, SAME_CORE_ROW, 0, 0)
     recv_b = lax.ppermute(recv_a, "core", SWAP)
-    partial = product(recv_a, recv_b, *arrange(slots, held))
+    partial = product(slots, recv_a, recv_b, held, row_sums(slots, held))
     received = lax.all_to_all(partial, COL, 0, 0)
     hidden, terms = nodes(received, weight, bias[None], cotangent)
     own_terms = jnp.sum(lax.all_to_all(terms, PLANE, 0, 0), axis=0)

time: 95.7 us -> 93.7 us (0.979)
  Pallas kernels: 12.8 us -> 9.92 us
  blocking collectives: 79 us -> 80 us
    all_to_all x1, blocking collectives: 29.5 us -> 31.7 us  [body(): recv_a = lax.all_to_all(send, SAME_CORE_ROW, 0, 0)]
    pallas_call x1, Pallas kernels: 4.48 us -> 2.77 us  [degrees(): pl.pallas_call(degree_kernel, in_specs=[smem, smem, hbm, hbm, hbm], out_s...]
    all_to_all x1, blocking collectives: 15.7 us -> 14.6 us  [body(): received = lax.all_to_all(partial, COL, 0, 0)]
    pallas_call x2, Pallas kernels: 6.71 us -> 5.59 us  [the longest x1 3.2 us: product(): pl.pallas_call(product_kernel, in_specs=[pl.BlockSpec(memory_space=pltpu....]
  transfers between devices with their start and end apart: 1 -> 1, of which waited for: 0 -> 0; matrix products, arithmetic and copies ran while one was open for 0% -> 0% of each run, Pallas kernels for 4% -> 3%
where the time goes in v4:
time: 93.7 us; the launch traced here: 93.3 us
  blocking collectives  80 us (85%)
  Pallas kernels  9.92 us (11%)
  starting transfers between devices  1.74 us (2%)
  between operations  1.34 us (1%)
    all_to_all x1, blocking collectives, body(): recv_a = lax.all_to_all(send, SAME_CORE_ROW, 0, 0)  31.7 us
    all_to_all x2, blocking collectives, gather(): lax.all_to_all(jnp.broadcast_to(x[None], (count,) + x.shape), axes, 0, 0)  22.1 us
    all_to_all x1, blocking collectives, body(): received = lax.all_to_all(partial, COL, 0, 0)  14.6 us
    all_to_all x1, blocking collectives, body(): own_terms = jnp.sum(lax.all_to_all(terms, PLANE, 0, 0), axis=0)  11.6 us
    pallas_call x1, Pallas kernels, product(): pl.pallas_call(product_kernel, in_specs=[pl.BlockSpec(memory_space=pltpu....  3.2 us
    pallas_call x1, Pallas kernels, degrees(): pl.pallas_call(degree_kernel, in_specs=[smem, smem, hbm, hbm, hbm], out_s...  2.77 us
    pallas_call x1, Pallas kernels, row_sums(): pl.pallas_call(row_sum_kernel, in_specs=[pl.BlockSpec(memory_space=pltpu....  2.39 us
  transfers between devices with their start and end apart: 1, of which 0 were waited for; matrix products, arithmetic and copies ran while one was open for 0% of the time, Pallas kernels for 3%

profile of v4, /device:TPU:1, one launch (start us, length us, event | category | flops | bytes accessed | tf_op | source)
XLA Modules:
  0.0 93.3 jit_solution(6367923622670707057)
XLA Ops:
  1.3 2.8 %degrees.1 = (bf16[16,160,128]{2,1,0:T(8,128)(2,1)S(1)}, s32[1,256]{1,0:T(1,128)S(1)}, bf16[257,128,128]{2,1,0:T(8,128)(2,1)S(1)}) custom-call(s32[1,1]{1,0:T(1,128)S(6)} %copy.13.count, s32[256]{0:T(256)} %perm.1, s32[2,256]{1,0:T(2,128)} %bitcast.6, bf16[128,128]{1,0:T(8,128)(2,1)} %feats_hbm.1, bf16[256,128,128]{2,1,0:T(8,128)(2,1)} %bitcast.5), custom_call_target="tpu_custom_call" | custom-call | tf_op jit(solution)/shard_map/degrees/pallas_call | solution.py:95
  4.1 31.7 %all_to_all.25.recv_a = bf16[16,160,128]{2,1,0:T(8,128)(2,1)S(1)} all-to-all(bf16[16,160,128]{2,1,0:T(8,128)(2,1)S(1)} %get-tuple-element.11), channel_id=1, replica_groups=mesh['z'=8,'y_lo'=2,'core'=2,'y_hi'=2,'x'=4] {'z','y_lo'}, dimensions={0} | all-to-all | bytes 1310720 | tf_op jit(solution)/shard_map/all_to_all | solution.py:254
  35.8 1.7 %collective-permute-start = (bf16[16,160,128]{2,1,0:T(8,128)(2,1)S(1)}, bf16[16,160,128]{2,1,0:T(8,128)(2,1)S(1)}, u32[]{:S(2)}, u32[]{:S(2)}) collective-permute-start(bf16[16,160,128]{2,1,0:T(8,128)(2,1)S(1)} %all_to_all.25.recv_a), channel_id=1, source_target_pairs={{0,8},{8,0},{1,9},{9,1},{2,10},{10,2},{3,11},{11,3},{4,12},{12,4},... | collective-permute-start | bytes 1966088 | tf_op jit(solution)/shard_map/ppermute | solution.py:255
  37.5 0.0 copy-start
  37.5 0.0 copy-start.1
  37.5 0.0 copy-start.2
  37.5 2.4 %row_sums.1.sums = bf16[8,16,128]{2,1,0:T(8,128)(2,1)S(1)} custom-call(s32[1,256]{1,0:T(1,128)S(1)} %get-tuple-element.10.slots, bf16[257,128,128]{2,1,0:T(8,128)(2,1)S(1)} %get-tuple-element.12.tiles), custom_call_target="tpu_custom_call" | custom-call | bytes 6291456 | tf_op jit(solution)/shard_map/row_sums/pallas_call | solution.py:130
  39.9 0.0 collective-permute-done.recv_b
  39.9 3.2 %product.1 = bf16[8,144,128]{2,1,0:T(8,128)(2,1)S(1)} custom-call(s32[1,256]{1,0:T(1,128)S(1)} %get-tuple-element.10.slots, bf16[16,160,128]{2,1,0:T(8,128)(2,1)S(1)} %all_to_all.25.recv_a, bf16[16,160,128]{2,1,0:T(8,128)(2,1)S(1)} %collective-permute-done.recv_b, bf16[257,128,128]{2,1,0:T(8,128)(2,1)S(1)} %get-tuple-element.12.tiles, ...), custom_call_target="tpu_custom_call" | custom-call | tf_op jit(solution)/shard_map/product/pallas_call | solution.py:176
  43.1 14.6 %all_to_all.26.parts = bf16[8,144,128]{2,1,0:T(8,128)(2,1)S(1)} all-to-all(bf16[8,144,128]{2,1,0:T(8,128)(2,1)S(1)} %product.1), channel_id=1, replica_groups=mesh['z'=8,'y_lo'=2,'core'=2,'y_hi'=2,'x'=4] {'y_hi','x'}, dimensions={0} | all-to-all | bytes 589824 | tf_op jit(solution)/shard_map/all_to_all | solution.py:257
  57.7 0.0 copy-done
  57.7 0.0 copy-done.1
  57.7 0.0 copy-done.2
  57.7 0.9 nodes.1
  58.6 11.6 %all_to_all.27 = f32[32,9,1,128]{3,2,1,0:T(1,128)S(1)} all-to-all(f32[32,9,1,128]{3,2,1,0:T(1,128)S(1)} %get-tuple-element.14), channel_id=1, replica_groups=mesh['z'=8,'y_lo'=2,'core'=2,'y_hi'=2,'x'=4] {'y_lo','core','y_hi','x'}, dimensions={0} | all-to-all | bytes 294912 | tf_op jit(solution)/shard_map/all_to_all | solution.py:259
  70.2 0.1 reduce_sum.18
  70.4 9.4 %all_to_all.28 = f32[8,9,1,128]{3,2,1,0:T(1,128)S(1)} all-to-all(f32[8,9,1,128]{3,2,1,0:T(1,128)S(1)} %broadcast_in_dim.7), channel_id=1, replica_groups=mesh['z'=8,'y_lo'=2,'core'=2,'y_hi'=2,'x'=4] {'z'}, dimensions={0} | all-to-all | bytes 73728 | tf_op jit(solution)/shard_map/all_to_all | solution.py:244
  79.8 0.1 broadcast_in_dim.8
  79.9 12.7 %all_to_all.29.every = f32[32,9,1,128]{3,2,1,0:T(1,128)S(1)} all-to-all(f32[32,9,1,128]{3,2,1,0:T(1,128)S(1)} %broadcast_in_dim.8), channel_id=1, replica_groups=mesh['z'=8,'y_lo'=2,'core'=2,'y_hi'=2,'x'=4] {'y_lo','core','y_hi','x'}, dimensions={0} | all-to-all | bytes 294912 | tf_op jit(solution)/shard_map/all_to_all | solution.py:244
  92.6 0.7 finish.1
  (3 shorter events, 0.1 us)
Async XLA Ops:
  35.8 4.1 %collective-permute-start = (bf16[16,160,128]{2,1,0:T(8,128)(2,1)S(1)}, bf16[16,160,128]{2,1,0:T(8,128)(2,1)S(1)}, u32[]{:S(2)}, u32[]{:S(2)}) collective-permute-start(bf16[16,160,128]{2,1,0:T(8,128)(2,1)S(1)} %all_to_all.25.recv_a), channel_id=1, source_target_pairs={{0,8},{8,0},{1,9},{9,1},{2,10},{10,2},{3,11},{11,3},{4,12},{12,4},... | collective-permute-start | bytes 1966088 | tf_op jit(solution)/shard_map/ppermute | solution.py:255
  37.5 20.2 %copy-start = (bf16[128,256]{1,0:T(8,128)(2,1)S(1)}, bf16[128,256]{1,0:T(8,128)(2,1)}, u32[]{:S(2)}) copy-start(bf16[128,256]{1,0:T(8,128)(2,1)} %weight.1) | copy-start | bytes 196612
  37.5 20.2 %copy-start.1 = (bf16[128,256]{1,0:T(8,128)(2,1)S(1)}, bf16[128,256]{1,0:T(8,128)(2,1)}, u32[]{:S(2)}) copy-start(bf16[128,256]{1,0:T(8,128)(2,1)} %cotangent.1) | copy-start | bytes 196612
  37.5 20.2 %copy-start.2 = (f32[256]{0:T(256)S(1)}, f32[256]{0:T(256)}, u32[]{:S(2)}) copy-start(f32[256]{0:T(256)} %param.10) | copy-start | bytes 3076

commit v5 on v4

--- a/solution.py
+++ b/solution.py
@@ -10,32 +10,41 @@
 ROW = ("z", "y_lo", "core")
 COL = ("y_hi", "x")
 SAME_CORE_ROW = ("z", "y_lo")
-PLANE = ("y_lo", "core", "y_hi", "x")
+NEAR = ("y_lo", "core", "x")
+FAR = ("z", "y_hi")
 SWAP = [(0, 1), (1, 0)]
 CHUNK = 16
 F32 = jnp.float32
 BF16 = jnp.bfloat16
 
 
-def degree_kernel(count, perm, pos_hbm, feats_hbm, tiles_hbm, send_ref, slot_ref, tiles, pos, feats, sums, sem, small):
+def degree_kernel(
+    count, perm_hbm, pos_hbm, feats_hbm, tiles_hbm, send_ref, slot_ref, tiles,
+    perm, pos, feats, sums, sem, small,
+):
     steps = 256 // CHUNK
 
     def chunk_copy(step):
         part = pl.ds(step * CHUNK, CHUNK)
         return pltpu.make_async_copy(tiles_hbm.at[part], tiles.at[part], sem.at[step])
 
-    pos_copy = pltpu.make_async_copy(pos_hbm, pos, small.at[0])
-    feats_copy = pltpu.make_async_copy(feats_hbm, feats, small.at[1])
+    perm_copy = pltpu.make_async_copy(perm_hbm, perm, small.at[0])
+    pos_copy = pltpu.make_async_copy(pos_hbm, pos, small.at[1])
+    feats_copy = pltpu.make_async_copy(feats_hbm, feats, small.at[2])
     pos_copy.start()
+    perm_copy.start()
     live_count = count[0, 0]
-    for step in range(steps):
-
+
+    @pl.loop(0, steps)
+    def _(step):
         @pl.when(step * CHUNK < live_count)
         def _():
             chunk_copy(step).start()
 
     feats_copy.start()
+    tiles[256] = jnp.zeros((128, 128), BF16)
     row, col, core = lax.axis_index(ROW), lax.axis_index(COL), lax.axis_index("core")
+    perm_copy.wait()
     pos_copy.wait()
     own_row = jnp.zeros((1, 256), jnp.int32)
     own_col = jnp.zeros((1, 256), jnp.int32)
@@ -57,7 +66,6 @@
     )
     found = found[0:1, :].astype(jnp.int32)
     slot_ref[...] = jnp.where(found == 0, 256, found - 1)
-    tiles[256] = jnp.zeros((128, 128), BF16)
 
     @pl.loop(0, steps)
     def _(step):
@@ -88,20 +96,20 @@
         send_ref[m, 128:160, :] = col_part.astype(BF16)
 
 
-def degrees(count, perm, pos, features, packed):
-    smem = pl.BlockSpec(memory_space=pltpu.SMEM)
+def degrees(*arrays):
     vmem = pl.BlockSpec(memory_space=pltpu.VMEM)
     hbm = pl.BlockSpec(memory_space=pltpu.HBM)
     return pl.pallas_call(
         degree_kernel,
-        in_specs=[smem, smem, hbm, hbm, hbm],
+        in_specs=[pl.BlockSpec(memory_space=pltpu.SMEM)] + [hbm] * 4,
         out_specs=[vmem, vmem, vmem],
         scratch_shapes=[
+            pltpu.SMEM((256,), jnp.int32),
             pltpu.VMEM((2, 256), jnp.int32),
             pltpu.VMEM((128, 128), BF16),
             pltpu.VMEM((256, 128), F32),
             pltpu.SemaphoreType.DMA((256 // CHUNK,)),
-            pltpu.SemaphoreType.DMA((2,)),
+            pltpu.SemaphoreType.DMA((3,)),
         ],
         out_shape=[
             jax.ShapeDtypeStruct((16, 160, 128), BF16),
@@ -110,7 +118,7 @@
         ],
         compiler_params=pltpu.CompilerParams(vmem_limit_bytes=16 << 20),
         name="degrees",
-    )(count, perm, pos, features, packed)
+    )(*arrays)
 
 
 def row_sum_kernel(slots, tiles, sums_ref):
@@ -198,11 +206,13 @@
         aggregated, grad, (((0,), (0,)), ((), ())), preferred_element_type=F32
     )
     bias_part = jnp.sum(grad.astype(F32), axis=0, keepdims=True)
-    for k in range(32):
-        half, f = k // 16, (k % 16) * 8
-        for s in range(8):
-            terms_ref[k, s, :, :] = weight_part[f + s : f + s + 1, half * 128 : half * 128 + 128]
-        terms_ref[k, 8, :, :] = (
+    for k in range(16):
+        for half in range(2):
+            for f in range(8):
+                terms_ref[k, half * 8 + f, :, :] = weight_part[
+                    k * 8 + f : k * 8 + f + 1, half * 128 : half * 128 + 128
+                ]
+        terms_ref[k, 16, :, :] = (
             bias_part[:, k * 128 : k * 128 + 128] if k < 2 else jnp.zeros((1, 128), F32)
         )
 
@@ -212,7 +222,7 @@
         node_kernel,
         out_shape=[
             jax.ShapeDtypeStruct((128, 256), BF16),
-            jax.ShapeDtypeStruct((32, 9, 1, 128), F32),
+            jax.ShapeDtypeStruct((16, 17, 1, 128), F32),
         ],
         compiler_params=pltpu.CompilerParams(vmem_limit_bytes=16 << 20),
         name="nodes",
@@ -220,12 +230,14 @@
 
 
 def finish_kernel(every, weight_ref, bias_ref):
-    for k in range(32):
-        half, f = k // 16, (k % 16) * 8
-        for s in range(8):
-            weight_ref[f + s : f + s + 1, half * 128 : half * 128 + 128] = every[k, s, :, :]
+    for k in range(16):
+        for half in range(2):
+            for f in range(8):
+                weight_ref[k * 8 + f : k * 8 + f + 1, half * 128 : half * 128 + 128] = every[
+                    k, half * 8 + f, :, :
+                ]
     for k in range(2):
-        bias_ref[:, k * 128 : k * 128 + 128] = every[k, 8, :, :]
+        bias_ref[:, k * 128 : k * 128 + 128] = every[k, 16, :, :]
 
 
 def finish(every):
@@ -256,9 +268,9 @@
     partial = product(slots, recv_a, recv_b, held, row_sums(slots, held))
     received = lax.all_to_all(partial, COL, 0, 0)
     hidden, terms = nodes(received, weight, bias[None], cotangent)
-    own_terms = jnp.sum(lax.all_to_all(terms, PLANE, 0, 0), axis=0)
-    total = jnp.sum(gather(own_terms, ("z",), 8), axis=0) * lax.rsqrt(F32(32768.0))
-    weight_grad, bias_grad = finish(gather(total, PLANE, 32))
+    own_terms = jnp.sum(lax.all_to_all(terms, NEAR, 0, 0), axis=0)
+    total = jnp.sum(gather(own_terms, FAR, 16), axis=0) * lax.rsqrt(F32(32768.0))
+    weight_grad, bias_grad = finish(gather(total, NEAR, 16))
     return hidden, weight_grad, bias_grad[0]
 
 

time: 93.7 us -> 91.9 us (0.981)
  starting transfers between devices: 1.74 us -> 0.01 us
    all_to_all x1, blocking collectives: 11.6 us -> 9.68 us  [body(): own_terms = jnp.sum(lax.all_to_all(terms, NEAR, 0, 0), axis=0)]
    ppermute x1, starting transfers between devices: 1.74 us -> 0.01 us  [body(): recv_b = lax.ppermute(recv_a, 'core', SWAP)]
    all_to_all x2, blocking collectives: 22.1 us -> 23.6 us  [gather(): lax.all_to_all(jnp.broadcast_to(x[None], (count,) + x.shape), axes, 0, 0)]
where the time goes in v5:
time: 91.9 us; the launch traced here: 91.3 us
  blocking collectives  79.5 us (87%)
  Pallas kernels  10.1 us (11%)
  between operations  1.35 us (1%)
    all_to_all x1, blocking collectives, body(): recv_a = lax.all_to_all(send, SAME_CORE_ROW, 0, 0)  31.6 us
    all_to_all x2, blocking collectives, gather(): lax.all_to_all(jnp.broadcast_to(x[None], (count,) + x.shape), axes, 0, 0)  23.6 us
    all_to_all x1, blocking collectives, body(): received = lax.all_to_all(partial, COL, 0, 0)  14.6 us
    all_to_all x1, blocking collectives, body(): own_terms = jnp.sum(lax.all_to_all(terms, NEAR, 0, 0), axis=0)  9.68 us
    pallas_call x1, Pallas kernels, product(): pl.pallas_call(product_kernel, in_specs=[pl.BlockSpec(memory_space=pltpu....  3.2 us
    pallas_call x1, Pallas kernels, degrees(): pl.pallas_call(degree_kernel, in_specs=[pl.BlockSpec(memory_space=pltpu.S...  2.92 us
    pallas_call x1, Pallas kernels, row_sums(): pl.pallas_call(row_sum_kernel, in_specs=[pl.BlockSpec(memory_space=pltpu....  2.4 us
  transfers between devices with their start and end apart: 1, of which 0 were waited for; matrix products, arithmetic and copies ran while one was open for 0% of the time, Pallas kernels for 3%

profile of v5, /device:TPU:1, one launch (start us, length us, event | category | flops | bytes accessed | tf_op | source)
XLA Modules:
  0.0 91.3 jit_solution(14481830956072511235)
XLA Ops:
  1.3 2.9 %degrees.1 = (bf16[16,160,128]{2,1,0:T(8,128)(2,1)S(1)}, s32[1,256]{1,0:T(1,128)S(1)}, bf16[257,128,128]{2,1,0:T(8,128)(2,1)S(1)}) custom-call(s32[1,1]{1,0:T(1,128)S(6)} %copy.13.count, s32[256]{0:T(256)} %perm_hbm.1, s32[2,256]{1,0:T(2,128)} %bitcast.6, bf16[128,128]{1,0:T(8,128)(2,1)} %feats_hbm.1, bf16[256,128,128]{2,1,0:T(8,128)(2,1)} %bitcast.5), custom_call_target="tpu_custom_call" | custom-call | tf_op jit(solution)/shard_map/degrees/pallas_call | solution.py:102
  4.2 31.6 %all_to_all.25.recv_a = bf16[16,160,128]{2,1,0:T(8,128)(2,1)S(1)} all-to-all(bf16[16,160,128]{2,1,0:T(8,128)(2,1)S(1)} %get-tuple-element.11), channel_id=1, replica_groups=mesh['z'=8,'y_lo'=2,'core'=2,'y_hi'=2,'x'=4] {'z','y_lo'}, dimensions={0} | all-to-all | bytes 1310720 | tf_op jit(solution)/shard_map/all_to_all | solution.py:266
  35.8 0.0 collective-permute-start
  35.8 0.0 copy-start
  35.8 0.0 copy-start.1
  35.8 0.0 copy-start.2
  35.8 2.4 %row_sums.1.sums = bf16[8,16,128]{2,1,0:T(8,128)(2,1)S(1)} custom-call(s32[1,256]{1,0:T(1,128)S(1)} %get-tuple-element.10.slots, bf16[257,128,128]{2,1,0:T(8,128)(2,1)S(1)} %get-tuple-element.12.tiles), custom_call_target="tpu_custom_call" | custom-call | bytes 6291456 | tf_op jit(solution)/shard_map/row_sums/pallas_call | solution.py:138
  38.2 0.0 collective-permute-done.recv_b
  38.2 3.2 %product.1 = bf16[8,144,128]{2,1,0:T(8,128)(2,1)S(1)} custom-call(s32[1,256]{1,0:T(1,128)S(1)} %get-tuple-element.10.slots, bf16[16,160,128]{2,1,0:T(8,128)(2,1)S(1)} %all_to_all.25.recv_a, bf16[16,160,128]{2,1,0:T(8,128)(2,1)S(1)} %collective-permute-done.recv_b, bf16[257,128,128]{2,1,0:T(8,128)(2,1)S(1)} %get-tuple-element.12.tiles, ...), custom_call_target="tpu_custom_call" | custom-call | tf_op jit(solution)/shard_map/product/pallas_call | solution.py:184
  41.4 14.6 %all_to_all.26.parts = bf16[8,144,128]{2,1,0:T(8,128)(2,1)S(1)} all-to-all(bf16[8,144,128]{2,1,0:T(8,128)(2,1)S(1)} %product.1), channel_id=1, replica_groups=mesh['z'=8,'y_lo'=2,'core'=2,'y_hi'=2,'x'=4] {'y_hi','x'}, dimensions={0} | all-to-all | bytes 589824 | tf_op jit(solution)/shard_map/all_to_all | solution.py:269
  56.0 0.0 copy-done
  56.0 0.0 copy-done.1
  56.0 0.0 copy-done.2
  56.0 0.9 nodes.1
  56.9 9.7 %all_to_all.27 = f32[16,17,1,128]{3,2,1,0:T(1,128)S(1)} all-to-all(f32[16,17,1,128]{3,2,1,0:T(1,128)S(1)} %get-tuple-element.14), channel_id=1, replica_groups=mesh['z'=8,'y_lo'=2,'core'=2,'y_hi'=2,'x'=4] {'y_lo','core','x'}, dimensions={0} | all-to-all | bytes 278528 | tf_op jit(solution)/shard_map/all_to_all | solution.py:271
  66.6 0.1 reduce_sum.18
  66.7 0.1 broadcast_in_dim.7
  66.8 13.0 %all_to_all.28 = f32[16,17,1,128]{3,2,1,0:T(1,128)S(1)} all-to-all(f32[16,17,1,128]{3,2,1,0:T(1,128)S(1)} %broadcast_in_dim.7), channel_id=1, replica_groups=mesh['z'=8,'y_lo'=2,'core'=2,'y_hi'=2,'x'=4] {'z','y_hi'}, dimensions={0} | all-to-all | bytes 278528 | tf_op jit(solution)/shard_map/all_to_all | solution.py:256
  79.8 0.1 reduce_sum.19
  79.9 0.1 broadcast_in_dim.8
  80.0 10.7 %all_to_all.29.every = f32[16,17,1,128]{3,2,1,0:T(1,128)S(1)} all-to-all(f32[16,17,1,128]{3,2,1,0:T(1,128)S(1)} %broadcast_in_dim.8), channel_id=1, replica_groups=mesh['z'=8,'y_lo'=2,'core'=2,'y_hi'=2,'x'=4] {'y_lo','core','x'}, dimensions={0} | all-to-all | bytes 278528 | tf_op jit(solution)/shard_map/all_to_all | solution.py:256
  90.6 0.7 finish.1
  (1 shorter events, 0.0 us)
Async XLA Ops:
  35.8 2.4 %collective-permute-start = (bf16[16,160,128]{2,1,0:T(8,128)(2,1)S(1)}, bf16[16,160,128]{2,1,0:T(8,128)(2,1)S(1)}, u32[]{:S(2)}, u32[]{:S(2)}) collective-permute-start(bf16[16,160,128]{2,1,0:T(8,128)(2,1)S(1)} %all_to_all.25.recv_a), channel_id=1, source_target_pairs={{0,8},{8,0},{1,9},{9,1},{2,10},{10,2},{3,11},{11,3},{4,12},{12,4},... | collective-permute-start | bytes 1966088 | tf_op jit(solution)/shard_map/ppermute | solution.py:267
  35.8 20.3 %copy-start = (bf16[128,256]{1,0:T(8,128)(2,1)S(1)}, bf16[128,256]{1,0:T(8,128)(2,1)}, u32[]{:S(2)}) copy-start(bf16[128,256]{1,0:T(8,128)(2,1)} %weight.1) | copy-start | bytes 196612
  35.8 20.3 %copy-start.1 = (bf16[128,256]{1,0:T(8,128)(2,1)S(1)}, bf16[128,256]{1,0:T(8,128)(2,1)}, u32[]{:S(2)}) copy-start(bf16[128,256]{1,0:T(8,128)(2,1)} %cotangent.1) | copy-start | bytes 196612
  35.8 20.3 %copy-start.2 = (f32[256]{0:T(256)S(1)}, f32[256]{0:T(256)}, u32[]{:S(2)}) copy-start(f32[256]{0:T(256)} %param.10) | copy-start | bytes 3076

commit v6 on v5

--- a/solution.py
+++ b/solution.py
@@ -122,11 +122,11 @@
 
 
 def row_sum_kernel(slots, tiles, sums_ref):
-    @pl.loop(0, 8)
-    def _(i):
+    for i in range(8):
         total = jnp.zeros((128, 128), F32)
-        for place in range(32):
-            total += tiles[slots[0, i * 32 + place]].astype(F32)
+        for place in range(0, 32, 2):
+            one, two = slots[0, i * 32 + place], slots[0, i * 32 + place + 1]
+            total += (tiles[one] + tiles[two]).astype(F32)
         sums = jnp.broadcast_to(jnp.sum(total.T, axis=0, keepdims=True), (8, 128))
         high = sums.astype(BF16)
         low = (sums - high.astype(F32)).astype(BF16)
@@ -140,56 +140,76 @@
         in_specs=[pl.BlockSpec(memory_space=pltpu.SMEM), vmem],
         out_specs=vmem,
         out_shape=pltpu.VMEM((8, 16, 128), BF16),
-        cost_estimate=pl.CostEstimate(flops=0, bytes_accessed=6 << 20, transcendentals=0),
+        cost_estimate=pl.CostEstimate(flops=0, bytes_accessed=3 << 20, transcendentals=0),
         compiler_params=pltpu.CompilerParams(vmem_limit_bytes=16 << 20),
         name="row_sums",
     )(slots, tiles)
 
 
-def product_kernel(slots, recv_a, recv_b, tiles, sums, out, rhs, acc):
-    from_a = jnp.sum(recv_a[:, 128:160, :].astype(F32), axis=0)
-    from_b = jnp.sum(recv_b[:, 128:160, :].astype(F32), axis=0)
-    degree = 1.0 + from_a + jnp.concatenate([from_b[16:32], from_b[0:16]], axis=0)
-    scale = jnp.concatenate([lax.rsqrt(degree), jnp.zeros((96, 128), F32)], axis=0).T
-    for part in range(4):
+def cell_part(slots, tiles, recv, scale, rhs, first):
+    terms = []
+    for part in range(2):
         for b in range(part * 8, part * 8 + 8):
-            feat = recv_a[b, 0:128, :] if b < 16 else recv_b[b - 16, 0:128, :]
-            scaled = scale[:, b : b + 1] * feat.astype(F32)
+            scaled = scale[:, first + b : first + b + 1] * recv[b, 0:128, :].astype(F32)
             rhs[b * 128 : b * 128 + 128, :] = scaled.astype(BF16)
         dense = jnp.concatenate(
             [
                 jnp.concatenate(
-                    [tiles[slots[0, i * 32 + part * 8 + q]] for q in range(8)], axis=1
+                    [tiles[slots[0, i * 32 + first + part * 8 + q]] for q in range(8)], axis=1
                 )
                 for i in range(8)
             ],
             axis=0,
         )
-        term = jnp.dot(
-            dense, rhs[part * 1024 : part * 1024 + 1024, :], preferred_element_type=F32
-        )
-        if part == 0:
-            acc[...] = term
-        elif part < 3:
-            acc[...] += term
-        else:
-            total = (acc[...] + term).astype(BF16)
+        block = rhs[part * 1024 : part * 1024 + 1024, :]
+        terms.append(jnp.dot(dense, block, preferred_element_type=F32))
+    return terms
+
+
+def near_kernel(slots, deg_a, deg_b, recv, tiles, acc, scale_ref, rhs):
+    from_b = deg_b[...]
+    degree = 1.0 + deg_a[...] + jnp.concatenate([from_b[16:32], from_b[0:16]], axis=0)
+    scale = jnp.concatenate([lax.rsqrt(degree), jnp.zeros((96, 128), F32)], axis=0).T
+    scale_ref[...] = scale
+    first, second = cell_part(slots, tiles, recv, scale, rhs, 0)
+    acc[...] = first
+    acc[...] += second
+
+
+def near_product(*arrays):
+    vmem = pl.BlockSpec(memory_space=pltpu.VMEM)
+    return pl.pallas_call(
+        near_kernel,
+        in_specs=[pl.BlockSpec(memory_space=pltpu.SMEM)] + [vmem] * 4,
+        out_specs=[vmem, vmem],
+        scratch_shapes=[pltpu.VMEM((2048, 128), BF16)],
+        out_shape=[pltpu.VMEM((1024, 128), F32), pltpu.VMEM((128, 128), F32)],
+        cost_estimate=pl.CostEstimate(flops=1 << 29, bytes_accessed=5 << 20, transcendentals=0),
+        compiler_params=pltpu.CompilerParams(vmem_limit_bytes=16 << 20),
+        name="near_product",
+    )(*arrays)
+
+
+def far_kernel(slots, recv, scale, acc, tiles, sums, out, rhs, half):
+    first, second = cell_part(slots, tiles, recv, scale, rhs, 16)
+    half[...] = acc[...] + first
+    total = (half[...] + second).astype(BF16)
     for i in range(8):
         out[i, 0:128, :] = total[i * 128 : i * 128 + 128, :]
         out[i, 128:144, :] = sums[i]
 
 
-def product(slots, recv_a, recv_b, tiles, sums):
+def far_product(*arrays):
     vmem = pl.BlockSpec(memory_space=pltpu.VMEM)
     return pl.pallas_call(
-        product_kernel,
-        in_specs=[pl.BlockSpec(memory_space=pltpu.SMEM), vmem, vmem, vmem, vmem],
+        far_kernel,
+        in_specs=[pl.BlockSpec(memory_space=pltpu.SMEM)] + [vmem] * 5,
         out_specs=vmem,
-        scratch_shapes=[pltpu.VMEM((4096, 128), BF16), pltpu.VMEM((1024, 128), F32)],
+        scratch_shapes=[pltpu.VMEM((2048, 128), BF16), pltpu.VMEM((1024, 128), F32)],
         out_shape=jax.ShapeDtypeStruct((8, 144, 128), BF16),
-        compiler_params=pltpu.CompilerParams(vmem_limit_bytes=24 << 20),
-        name="product",
-    )(slots, recv_a, recv_b, tiles, sums)
+        compiler_params=pltpu.CompilerParams(vmem_limit_bytes=16 << 20),
+        name="far_product",
+    )(*arrays)
 
 
 def node_kernel(parts, weight, bias, cotangent, hidden_ref, terms_ref):
@@ -264,8 +284,11 @@
     ]
     send, slots, held = degrees(tile_count, *in_hbm)
     recv_a = lax.all_to_all(send, SAME_CORE_ROW, 0, 0)
+    deg_a = jnp.sum(recv_a[:, 128:160, :].astype(F32), axis=0)
+    deg_b = lax.ppermute(deg_a, "core", SWAP)
     recv_b = lax.ppermute(recv_a, "core", SWAP)
-    partial = product(slots, recv_a, recv_b, held, row_sums(slots, held))
+    acc, scale = near_product(slots, deg_a, deg_b, recv_a, held)
+    partial = far_product(slots, recv_b, scale, acc, held, row_sums(slots, held))
     received = lax.all_to_all(partial, COL, 0, 0)
     hidden, terms = nodes(received, weight, bias[None], cotangent)
     own_terms = jnp.sum(lax.all_to_all(terms, NEAR, 0, 0), axis=0)

time: 91.9 us -> 92.8 us (level)
  starting transfers between devices: 0.01 us -> 2.27 us
  blocking collectives: 79.5 us -> 78 us
    all_to_all x1, blocking collectives: 31.6 us -> 29.4 us  [body(): recv_a = lax.all_to_all(send, SAME_CORE_ROW, 0, 0)]
    ppermute x1, starting transfers between devices: 0.01 us -> 2.18 us  [body(): recv_b = lax.ppermute(recv_a, 'core', SWAP)]
    pallas_call x1 -> x2, Pallas kernels: 3.2 us -> 4.08 us  [the longest x1 2.08 us: near_product(): pl.pallas_call(near_kernel, in_specs=[pl.BlockSpec(memory_space=pltpu.SME...]
  transfers between devices with their start and end apart: 1 -> 2, of which waited for: 0 -> 0; matrix products, arithmetic and copies ran while one was open for 0% -> 0% of each run, Pallas kernels for 3% -> 5%
where the time goes in v6:
time: 92.8 us; the launch traced here: 92.4 us
  blocking collectives  78 us (84%)
  Pallas kernels  10.4 us (11%)
  starting transfers between devices  2.27 us (2%)
  between operations  1.39 us (1%)
    all_to_all x1, blocking collectives, body(): recv_a = lax.all_to_all(send, SAME_CORE_ROW, 0, 0)  29.4 us
    all_to_all x2, blocking collectives, gather(): lax.all_to_all(jnp.broadcast_to(x[None], (count,) + x.shape), axes, 0, 0)  23.6 us
    all_to_all x1, blocking collectives, body(): received = lax.all_to_all(partial, COL, 0, 0)  14.7 us
    all_to_all x1, blocking collectives, body(): own_terms = jnp.sum(lax.all_to_all(terms, NEAR, 0, 0), axis=0)  10.2 us
    pallas_call x1, Pallas kernels, degrees(): pl.pallas_call(degree_kernel, in_specs=[pl.BlockSpec(memory_space=pltpu.S...  2.63 us
    ppermute x1, starting transfers between devices, body(): recv_b = lax.ppermute(recv_a, 'core', SWAP)  2.18 us
    pallas_call x1, Pallas kernels, row_sums(): pl.pallas_call(row_sum_kernel, in_specs=[pl.BlockSpec(memory_space=pltpu....  2.15 us
    pallas_call x1, Pallas kernels, near_product(): pl.pallas_call(near_kernel, in_specs=[pl.BlockSpec(memory_space=pltpu.SME...  2.08 us
  transfers between devices with their start and end apart: 2, of which 0 were waited for; matrix products, arithmetic and copies ran while one was open for 0% of the time, Pallas kernels for 5%

profile of v6, /device:TPU:1, one launch (start us, length us, event | category | flops | bytes accessed | tf_op | source)
XLA Modules:
  0.0 92.4 jit_solution(7531559381683122720)
XLA Ops:
  1.3 2.6 %degrees.1 = (bf16[16,160,128]{2,1,0:T(8,128)(2,1)S(1)}, s32[1,256]{1,0:T(1,128)S(1)}, bf16[257,128,128]{2,1,0:T(8,128)(2,1)S(1)}) custom-call(s32[1,1]{1,0:T(1,128)S(6)} %copy.13.count, s32[256]{0:T(256)} %perm_hbm.1, s32[2,256]{1,0:T(2,128)} %bitcast.6, bf16[128,128]{1,0:T(8,128)(2,1)} %feats_hbm.1, bf16[256,128,128]{2,1,0:T(8,128)(2,1)} %bitcast.5), custom_call_target="tpu_custom_call" | custom-call | tf_op jit(solution)/shard_map/degrees/pallas_call | solution.py:102
  3.9 29.4 %all_to_all.25.recv = bf16[16,160,128]{2,1,0:T(8,128)(2,1)S(1)} all-to-all(bf16[16,160,128]{2,1,0:T(8,128)(2,1)S(1)} %get-tuple-element.13), channel_id=1, replica_groups=mesh['z'=8,'y_lo'=2,'core'=2,'y_hi'=2,'x'=4] {'z','y_lo'}, dimensions={0} | all-to-all | bytes 1310720 | tf_op jit(solution)/shard_map/all_to_all | solution.py:286
  33.3 2.2 %collective-permute-start = (bf16[16,160,128]{2,1,0:T(8,128)(2,1)S(1)}, bf16[16,160,128]{2,1,0:T(8,128)(2,1)S(1)}, u32[]{:S(2)}, u32[]{:S(2)}) collective-permute-start(bf16[16,160,128]{2,1,0:T(8,128)(2,1)S(1)} %all_to_all.25.recv), channel_id=1, source_target_pairs={{0,8},{8,0},{1,9},{9,1},{2,10},{10,2},{3,11},{11,3},{4,12},{12,4},... | collective-permute-start | bytes 1966088 | tf_op jit(solution)/shard_map/ppermute | solution.py:289
  35.5 0.1 collective-permute-start.1
  35.6 2.1 %row_sums.1.sums = bf16[8,16,128]{2,1,0:T(8,128)(2,1)S(1)} custom-call(s32[1,256]{1,0:T(1,128)S(1)} %get-tuple-element.12.slots, bf16[257,128,128]{2,1,0:T(8,128)(2,1)S(1)} %get-tuple-element.14.tiles), custom_call_target="tpu_custom_call" | custom-call | bytes 3145728 | tf_op jit(solution)/shard_map/row_sums/pallas_call | solution.py:138
  37.8 0.0 copy-start
  37.8 0.0 copy-start.1
  37.8 0.0 copy-start.2
  37.8 0.0 collective-permute-done.1.deg_b
  37.8 2.1 %near_product.1 = (f32[1024,128]{1,0:T(8,128)S(1)}, f32[128,128]{1,0:T(8,128)S(1)}) custom-call(s32[1,256]{1,0:T(1,128)S(1)} %get-tuple-element.12.slots, f32[32,128]{1,0:T(8,128)S(1)} %convert_reduce_fusion.deg_a, f32[32,128]{1,0:T(8,128)S(1)} %collective-permute-done.1.deg_b, bf16[16,160,128]{2,1,0:T(8,128)(2,1)S(1)} %all_to_all.25.recv, ...), custom_call_target="tpu_custom_call" | custom-call | flops 536870912 | bytes 5242880 | tf_op jit(solution)/shard_map/near_product/pallas_call | solution.py:181
  39.9 0.0 collective-permute-done.recv
  39.9 2.0 %far_product.1 = bf16[8,144,128]{2,1,0:T(8,128)(2,1)S(1)} custom-call(s32[1,256]{1,0:T(1,128)S(1)} %get-tuple-element.12.slots, bf16[16,160,128]{2,1,0:T(8,128)(2,1)S(1)} %collective-permute-done.recv, f32[128,128]{1,0:T(8,128)S(1)} %get-tuple-element.15.scale, f32[1024,128]{1,0:T(8,128)S(1)} %get-tuple-element.16.acc, ...), custom_call_target="tpu_custom_call" | custom-call | tf_op jit(solution)/shard_map/far_product/pallas_call | solution.py:204
  41.9 14.7 %all_to_all.26.parts = bf16[8,144,128]{2,1,0:T(8,128)(2,1)S(1)} all-to-all(bf16[8,144,128]{2,1,0:T(8,128)(2,1)S(1)} %far_product.1), channel_id=1, replica_groups=mesh['z'=8,'y_lo'=2,'core'=2,'y_hi'=2,'x'=4] {'y_hi','x'}, dimensions={0} | all-to-all | bytes 589824 | tf_op jit(solution)/shard_map/all_to_all | solution.py:292
  56.6 0.0 copy-done
  56.6 0.0 copy-done.1
  56.6 0.9 nodes.1
  57.5 10.2 %all_to_all.27 = f32[16,17,1,128]{3,2,1,0:T(1,128)S(1)} all-to-all(f32[16,17,1,128]{3,2,1,0:T(1,128)S(1)} %get-tuple-element.18), channel_id=1, replica_groups=mesh['z'=8,'y_lo'=2,'core'=2,'y_hi'=2,'x'=4] {'y_lo','core','x'}, dimensions={0} | all-to-all | bytes 278528 | tf_op jit(solution)/shard_map/all_to_all | solution.py:294
  67.8 0.1 reduce_sum.28
  67.8 0.1 broadcast_in_dim.7
  67.9 13.0 %all_to_all.28 = f32[16,17,1,128]{3,2,1,0:T(1,128)S(1)} all-to-all(f32[16,17,1,128]{3,2,1,0:T(1,128)S(1)} %broadcast_in_dim.7), channel_id=1, replica_groups=mesh['z'=8,'y_lo'=2,'core'=2,'y_hi'=2,'x'=4] {'z','y_hi'}, dimensions={0} | all-to-all | bytes 278528 | tf_op jit(solution)/shard_map/all_to_all | solution.py:276
  80.9 0.1 reduce_sum.29
  81.0 0.1 broadcast_in_dim.8
  81.1 10.7 %all_to_all.29.every = f32[16,17,1,128]{3,2,1,0:T(1,128)S(1)} all-to-all(f32[16,17,1,128]{3,2,1,0:T(1,128)S(1)} %broadcast_in_dim.8), channel_id=1, replica_groups=mesh['z'=8,'y_lo'=2,'core'=2,'y_hi'=2,'x'=4] {'y_lo','core','x'}, dimensions={0} | all-to-all | bytes 278528 | tf_op jit(solution)/shard_map/all_to_all | solution.py:276
  91.8 0.7 finish.1
  (3 shorter events, 0.0 us)
Async XLA Ops:
  33.3 6.6 %collective-permute-start = (bf16[16,160,128]{2,1,0:T(8,128)(2,1)S(1)}, bf16[16,160,128]{2,1,0:T(8,128)(2,1)S(1)}, u32[]{:S(2)}, u32[]{:S(2)}) collective-permute-start(bf16[16,160,128]{2,1,0:T(8,128)(2,1)S(1)} %all_to_all.25.recv), channel_id=1, source_target_pairs={{0,8},{8,0},{1,9},{9,1},{2,10},{10,2},{3,11},{11,3},{4,12},{12,4},... | collective-permute-start | bytes 1966088 | tf_op jit(solution)/shard_map/ppermute | solution.py:289
  35.5 2.3 %collective-permute-start.1 = (f32[32,128]{1,0:T(8,128)S(1)}, f32[32,128]{1,0:T(8,128)S(1)}, u32[]{:S(2)}, u32[]{:S(2)}) collective-permute-start(f32[32,128]{1,0:T(8,128)S(1)} %convert_reduce_fusion.deg_a), channel_id=1, source_target_pairs={{0,8},{8,0},{1,9},{9,1},{2,10},{10,2},{3,11},{11,3},{4,12},{12,4},... | collective-permute-start | bytes 49160 | tf_op jit(solution)/shard_map/ppermute | solution.py:288
  37.8 18.9 %copy-start = (bf16[128,256]{1,0:T(8,128)(2,1)S(1)}, bf16[128,256]{1,0:T(8,128)(2,1)}, u32[]{:S(2)}) copy-start(bf16[128,256]{1,0:T(8,128)(2,1)} %weight.1) | copy-start | bytes 196612
  37.8 18.8 %copy-start.1 = (bf16[128,256]{1,0:T(8,128)(2,1)S(1)}, bf16[128,256]{1,0:T(8,128)(2,1)}, u32[]{:S(2)}) copy-start(bf16[128,256]{1,0:T(8,128)(2,1)} %cotangent.1) | copy-start | bytes 196612
  37.8 18.8 %copy-start.2 = (f32[256]{0:T(256)S(1)}, f32[256]{0:T(256)}, u32[]{:S(2)}) copy-start(f32[256]{0:T(256)} %param.10) | copy-start | bytes 3076

commit v7 on v5

--- a/solution.py
+++ b/solution.py
@@ -20,7 +20,7 @@
 
 def degree_kernel(
     count, perm_hbm, pos_hbm, feats_hbm, tiles_hbm, send_ref, slot_ref, tiles,
-    perm, pos, feats, sums, sem, small,
+    perm, pos, feats, sums, places, sem, small,
 ):
     steps = 256 // CHUNK
 
@@ -65,7 +65,9 @@
         preferred_element_type=F32,
     )
     found = found[0:1, :].astype(jnp.int32)
-    slot_ref[...] = jnp.where(found == 0, 256, found - 1)
+    places[...] = jnp.where(found == 0, 256, found - 1)
+    slot_copy = pltpu.make_async_copy(places, slot_ref, small.at[3])
+    slot_copy.start()
 
     @pl.loop(0, steps)
     def _(step):
@@ -90,6 +92,7 @@
     low = (sums[...] - high.astype(F32)).astype(BF16)
     col_part = jnp.dot(pick, high, preferred_element_type=F32)
     col_part += jnp.dot(pick, low, preferred_element_type=F32)
+    slot_copy.wait()
     feats_copy.wait()
     for m in range(16):
         send_ref[m, 0:128, :] = feats[...]
@@ -102,18 +105,19 @@
     return pl.pallas_call(
         degree_kernel,
         in_specs=[pl.BlockSpec(memory_space=pltpu.SMEM)] + [hbm] * 4,
-        out_specs=[vmem, vmem, vmem],
+        out_specs=[vmem, pl.BlockSpec(memory_space=pltpu.SMEM), vmem],
         scratch_shapes=[
             pltpu.SMEM((256,), jnp.int32),
             pltpu.VMEM((2, 256), jnp.int32),
             pltpu.VMEM((128, 128), BF16),
             pltpu.VMEM((256, 128), F32),
+            pltpu.VMEM((1, 256), jnp.int32),
             pltpu.SemaphoreType.DMA((256 // CHUNK,)),
-            pltpu.SemaphoreType.DMA((3,)),
+            pltpu.SemaphoreType.DMA((4,)),
         ],
         out_shape=[
             jax.ShapeDtypeStruct((16, 160, 128), BF16),
-            jax.ShapeDtypeStruct((1, 256), jnp.int32),
+            pltpu.SMEM((1, 256), jnp.int32),
             pltpu.VMEM((257, 128, 128), BF16),
         ],
         compiler_params=pltpu.CompilerParams(vmem_limit_bytes=16 << 20),
@@ -122,15 +126,22 @@
 
 
 def row_sum_kernel(slots, tiles, sums_ref):
+    ones = jnp.ones((16, 128), BF16)
+
     @pl.loop(0, 8)
     def _(i):
         total = jnp.zeros((128, 128), F32)
-        for place in range(32):
-            total += tiles[slots[0, i * 32 + place]].astype(F32)
-        sums = jnp.broadcast_to(jnp.sum(total.T, axis=0, keepdims=True), (8, 128))
+        for place in range(0, 32, 2):
+            one, two = slots[0, i * 32 + place], slots[0, i * 32 + place + 1]
+            total += (tiles[one] + tiles[two]).astype(F32)
+        high = total.astype(BF16)
+        low = (total - high.astype(F32)).astype(BF16)
+        dims = (((1,), (1,)), ((), ()))
+        sums = lax.dot_general(ones, high, dims, preferred_element_type=F32)
+        sums += lax.dot_general(ones, low, dims, preferred_element_type=F32)
         high = sums.astype(BF16)
         low = (sums - high.astype(F32)).astype(BF16)
-        sums_ref[i] = jnp.concatenate([high, low], axis=0)
+        sums_ref[i] = jnp.concatenate([high[0:8], low[0:8]], axis=0)
 
 
 def row_sums(slots, tiles):

time: 91.9 us -> 91.4 us (level)
  starting transfers between devices: 0.01 us -> 2.02 us
  Pallas kernels: 10.1 us -> 8.1 us
    ppermute x1, starting transfers between devices: 0.01 us -> 2.02 us  [body(): recv_b = lax.ppermute(recv_a, 'core', SWAP)]
    all_to_all x1, blocking collectives: 31.6 us -> 30.3 us  [body(): recv_a = lax.all_to_all(send, SAME_CORE_ROW, 0, 0)]
    all_to_all x1, blocking collectives: 14.6 us -> 15.8 us  [body(): received = lax.all_to_all(partial, COL, 0, 0)]
    pallas_call x1, Pallas kernels: 2.92 us -> 1.86 us  [degrees(): pl.pallas_call(degree_kernel, in_specs=[pl.BlockSpec(memory_space=pltpu.S...]
  transfers between devices with their start and end apart: 1 -> 1, of which waited for: 0 -> 0; matrix products, arithmetic and copies ran while one was open for 0% -> 0% of each run, Pallas kernels for 3% -> 2%
where the time goes in v7:
time: 91.4 us; the launch traced here: 91.3 us
  blocking collectives  79.5 us (87%)
  Pallas kernels  8.1 us (9%)
  starting transfers between devices  2.02 us (2%)
  between operations  1.34 us (1%)
    all_to_all x1, blocking collectives, body(): recv_a = lax.all_to_all(send, SAME_CORE_ROW, 0, 0)  30.3 us
    all_to_all x2, blocking collectives, gather(): lax.all_to_all(jnp.broadcast_to(x[None], (count,) + x.shape), axes, 0, 0)  23.6 us
    all_to_all x1, blocking collectives, body(): received = lax.all_to_all(partial, COL, 0, 0)  15.8 us
    all_to_all x1, blocking collectives, body(): own_terms = jnp.sum(lax.all_to_all(terms, NEAR, 0, 0), axis=0)  9.68 us
    pallas_call x1, Pallas kernels, product(): pl.pallas_call(product_kernel, in_specs=[pl.BlockSpec(memory_space=pltpu....  2.64 us
    pallas_call x1, Pallas kernels, row_sums(): pl.pallas_call(row_sum_kernel, in_specs=[pl.BlockSpec(memory_space=pltpu....  2.03 us
    ppermute x1, starting transfers between devices, body(): recv_b = lax.ppermute(recv_a, 'core', SWAP)  2.02 us
    pallas_call x1, Pallas kernels, degrees(): pl.pallas_call(degree_kernel, in_specs=[pl.BlockSpec(memory_space=pltpu.S...  1.86 us
  transfers between devices with their start and end apart: 1, of which 0 were waited for; matrix products, arithmetic and copies ran while one was open for 0% of the time, Pallas kernels for 2%

profile of v7, /device:TPU:1, one launch (start us, length us, event | category | flops | bytes accessed | tf_op | source)
XLA Modules:
  0.0 91.3 jit_solution(4352451463941863029)
XLA Ops:
  1.3 1.9 %degrees.1 = (bf16[16,160,128]{2,1,0:T(8,128)(2,1)S(1)}, s32[1,256]{1,0:T(1,128)S(4)}, bf16[257,128,128]{2,1,0:T(8,128)(2,1)S(1)}) custom-call(s32[1,1]{1,0:T(1,128)S(6)} %copy.13.count, s32[256]{0:T(256)} %perm_hbm.1, s32[2,256]{1,0:T(2,128)} %bitcast.6, bf16[128,128]{1,0:T(8,128)(2,1)} %feats_hbm.1, bf16[256,128,128]{2,1,0:T(8,128)(2,1)} %bitcast.5), custom_call_target="tpu_custom_call" | custom-call | tf_op jit(solution)/shard_map/degrees/pallas_call | solution.py:105
  3.1 30.3 %all_to_all.25.recv_a = bf16[16,160,128]{2,1,0:T(8,128)(2,1)S(1)} all-to-all(bf16[16,160,128]{2,1,0:T(8,128)(2,1)S(1)} %get-tuple-element.11), channel_id=1, replica_groups=mesh['z'=8,'y_lo'=2,'core'=2,'y_hi'=2,'x'=4] {'z','y_lo'}, dimensions={0} | all-to-all | bytes 1310720 | tf_op jit(solution)/shard_map/all_to_all | solution.py:277
  33.5 2.0 %collective-permute-start = (bf16[16,160,128]{2,1,0:T(8,128)(2,1)S(1)}, bf16[16,160,128]{2,1,0:T(8,128)(2,1)S(1)}, u32[]{:S(2)}, u32[]{:S(2)}) collective-permute-start(bf16[16,160,128]{2,1,0:T(8,128)(2,1)S(1)} %all_to_all.25.recv_a), channel_id=1, source_target_pairs={{0,8},{8,0},{1,9},{9,1},{2,10},{10,2},{3,11},{11,3},{4,12},{12,4},... | collective-permute-start | bytes 1966088 | tf_op jit(solution)/shard_map/ppermute | solution.py:278
  35.5 0.0 copy-start
  35.5 0.0 copy-start.1
  35.5 0.0 copy-start.2
  35.5 2.0 %row_sums.1.sums = bf16[8,16,128]{2,1,0:T(8,128)(2,1)S(1)} custom-call(s32[1,256]{1,0:T(1,128)S(4)} %get-tuple-element.10.slots, bf16[257,128,128]{2,1,0:T(8,128)(2,1)S(1)} %get-tuple-element.12.tiles), custom_call_target="tpu_custom_call" | custom-call | bytes 6291456 | tf_op jit(solution)/shard_map/row_sums/pallas_call | solution.py:149
  37.5 0.0 collective-permute-done.recv_b
  37.6 2.6 %product.1 = bf16[8,144,128]{2,1,0:T(8,128)(2,1)S(1)} custom-call(s32[1,256]{1,0:T(1,128)S(4)} %get-tuple-element.10.slots, bf16[16,160,128]{2,1,0:T(8,128)(2,1)S(1)} %all_to_all.25.recv_a, bf16[16,160,128]{2,1,0:T(8,128)(2,1)S(1)} %collective-permute-done.recv_b, bf16[257,128,128]{2,1,0:T(8,128)(2,1)S(1)} %get-tuple-element.12.tiles, ...), custom_call_target="tpu_custom_call" | custom-call | tf_op jit(solution)/shard_map/product/pallas_call | solution.py:195
  40.2 15.8 %all_to_all.26.parts = bf16[8,144,128]{2,1,0:T(8,128)(2,1)S(1)} all-to-all(bf16[8,144,128]{2,1,0:T(8,128)(2,1)S(1)} %product.1), channel_id=1, replica_groups=mesh['z'=8,'y_lo'=2,'core'=2,'y_hi'=2,'x'=4] {'y_hi','x'}, dimensions={0} | all-to-all | bytes 589824 | tf_op jit(solution)/shard_map/all_to_all | solution.py:280
  56.0 0.0 copy-done
  56.0 0.0 copy-done.1
  56.0 0.0 copy-done.2
  56.0 0.9 nodes.1
  56.9 9.7 %all_to_all.27 = f32[16,17,1,128]{3,2,1,0:T(1,128)S(1)} all-to-all(f32[16,17,1,128]{3,2,1,0:T(1,128)S(1)} %get-tuple-element.14), channel_id=1, replica_groups=mesh['z'=8,'y_lo'=2,'core'=2,'y_hi'=2,'x'=4] {'y_lo','core','x'}, dimensions={0} | all-to-all | bytes 278528 | tf_op jit(solution)/shard_map/all_to_all | solution.py:282
  66.6 0.1 reduce_sum.18
  66.7 0.1 broadcast_in_dim.7
  66.8 13.0 %all_to_all.28 = f32[16,17,1,128]{3,2,1,0:T(1,128)S(1)} all-to-all(f32[16,17,1,128]{3,2,1,0:T(1,128)S(1)} %broadcast_in_dim.7), channel_id=1, replica_groups=mesh['z'=8,'y_lo'=2,'core'=2,'y_hi'=2,'x'=4] {'z','y_hi'}, dimensions={0} | all-to-all | bytes 278528 | tf_op jit(solution)/shard_map/all_to_all | solution.py:267
  79.8 0.1 reduce_sum.19
  79.9 0.1 broadcast_in_dim.8
  79.9 10.7 %all_to_all.29.every = f32[16,17,1,128]{3,2,1,0:T(1,128)S(1)} all-to-all(f32[16,17,1,128]{3,2,1,0:T(1,128)S(1)} %broadcast_in_dim.8), channel_id=1, replica_groups=mesh['z'=8,'y_lo'=2,'core'=2,'y_hi'=2,'x'=4] {'y_lo','core','x'}, dimensions={0} | all-to-all | bytes 278528 | tf_op jit(solution)/shard_map/all_to_all | solution.py:267
  90.6 0.7 finish.1
  (1 shorter events, 0.0 us)
Async XLA Ops:
  33.5 4.1 %collective-permute-start = (bf16[16,160,128]{2,1,0:T(8,128)(2,1)S(1)}, bf16[16,160,128]{2,1,0:T(8,128)(2,1)S(1)}, u32[]{:S(2)}, u32[]{:S(2)}) collective-permute-start(bf16[16,160,128]{2,1,0:T(8,128)(2,1)S(1)} %all_to_all.25.recv_a), channel_id=1, source_target_pairs={{0,8},{8,0},{1,9},{9,1},{2,10},{10,2},{3,11},{11,3},{4,12},{12,4},... | collective-permute-start | bytes 1966088 | tf_op jit(solution)/shard_map/ppermute | solution.py:278
  35.5 20.5 %copy-start = (bf16[128,256]{1,0:T(8,128)(2,1)S(1)}, bf16[128,256]{1,0:T(8,128)(2,1)}, u32[]{:S(2)}) copy-start(bf16[128,256]{1,0:T(8,128)(2,1)} %weight.1) | copy-start | bytes 196612
  35.5 20.5 %copy-start.1 = (bf16[128,256]{1,0:T(8,128)(2,1)S(1)}, bf16[128,256]{1,0:T(8,128)(2,1)}, u32[]{:S(2)}) copy-start(bf16[128,256]{1,0:T(8,128)(2,1)} %cotangent.1) | copy-start | bytes 196612
  35.5 20.5 %copy-start.2 = (f32[256]{0:T(256)S(1)}, f32[256]{0:T(256)}, u32[]{:S(2)}) copy-start(f32[256]{0:T(256)} %param.10) | copy-start | bytes 3076

commit v8 on v7

--- a/solution.py
+++ b/solution.py
@@ -125,7 +125,7 @@
     )(*arrays)
 
 
-def row_sum_kernel(slots, tiles, sums_ref):
+def row_sum_kernel(slots, tiles, sums_ref, highs, lows):
     ones = jnp.ones((16, 128), BF16)
 
     @pl.loop(0, 8)
@@ -135,13 +135,18 @@
             one, two = slots[0, i * 32 + place], slots[0, i * 32 + place + 1]
             total += (tiles[one] + tiles[two]).astype(F32)
         high = total.astype(BF16)
-        low = (total - high.astype(F32)).astype(BF16)
-        dims = (((1,), (1,)), ((), ()))
-        sums = lax.dot_general(ones, high, dims, preferred_element_type=F32)
-        sums += lax.dot_general(ones, low, dims, preferred_element_type=F32)
-        high = sums.astype(BF16)
-        low = (sums - high.astype(F32)).astype(BF16)
-        sums_ref[i] = jnp.concatenate([high[0:8], low[0:8]], axis=0)
+        rows = pl.ds(pl.multiple_of(i * 128, 128), 128)
+        highs[rows, :] = high
+        lows[rows, :] = (total - high.astype(F32)).astype(BF16)
+
+    dims = (((1,), (1,)), ((), ()))
+    sums = lax.dot_general(ones, highs[...], dims, preferred_element_type=F32)
+    sums += lax.dot_general(ones, lows[...], dims, preferred_element_type=F32)
+    high = sums.astype(BF16)
+    low = (sums - high.astype(F32)).astype(BF16)
+    for i in range(8):
+        lanes = slice(i * 128, i * 128 + 128)
+        sums_ref[i] = jnp.concatenate([high[0:8, lanes], low[0:8, lanes]], axis=0)
 
 
 def row_sums(slots, tiles):
@@ -151,6 +156,7 @@
         in_specs=[pl.BlockSpec(memory_space=pltpu.SMEM), vmem],
         out_specs=vmem,
         out_shape=pltpu.VMEM((8, 16, 128), BF16),
+        scratch_shapes=[pltpu.VMEM((1024, 128), BF16), pltpu.VMEM((1024, 128), BF16)],
         cost_estimate=pl.CostEstimate(flops=0, bytes_accessed=6 << 20, transcendentals=0),
         compiler_params=pltpu.CompilerParams(vmem_limit_bytes=16 << 20),
         name="row_sums",
@@ -232,7 +238,7 @@
     return pl.pallas_call(
         node_kernel,
         out_shape=[
-            jax.ShapeDtypeStruct((128, 256), BF16),
+            pltpu.VMEM((128, 256), BF16),
             jax.ShapeDtypeStruct((16, 17, 1, 128), F32),
         ],
         compiler_params=pltpu.CompilerParams(vmem_limit_bytes=16 << 20),
@@ -240,7 +246,8 @@
     )(parts, weight, bias, cotangent)
 
 
-def finish_kernel(every, weight_ref, bias_ref):
+def finish_kernel(every, hidden, hidden_ref, weight_ref, bias_ref):
+    hidden_ref[...] = hidden[...]
     for k in range(16):
         for half in range(2):
             for f in range(8):
@@ -251,16 +258,17 @@
         bias_ref[:, k * 128 : k * 128 + 128] = every[k, 16, :, :]
 
 
-def finish(every):
+def finish(every, hidden):
     return pl.pallas_call(
         finish_kernel,
         out_shape=[
+            jax.ShapeDtypeStruct((128, 256), BF16),
             jax.ShapeDtypeStruct((128, 256), F32),
             jax.ShapeDtypeStruct((1, 256), F32),
         ],
         compiler_params=pltpu.CompilerParams(vmem_limit_bytes=16 << 20),
         name="finish",
-    )(every)
+    )(every, hidden)
 
 
 def gather(x, axes, count):
@@ -281,7 +289,7 @@
     hidden, terms = nodes(received, weight, bias[None], cotangent)
     own_terms = jnp.sum(lax.all_to_all(terms, NEAR, 0, 0), axis=0)
     total = jnp.sum(gather(own_terms, FAR, 16), axis=0) * lax.rsqrt(F32(32768.0))
-    weight_grad, bias_grad = finish(gather(total, NEAR, 16))
+    hidden, weight_grad, bias_grad = finish(gather(total, NEAR, 16), hidden)
     return hidden, weight_grad, bias_grad[0]
 
 

time: 91.4 us -> 91.1 us (level)
  blocking collectives: 79.5 us -> 78.4 us
    all_to_all x1, blocking collectives: 30.3 us -> 28.5 us  [body(): recv_a = lax.all_to_all(send, SAME_CORE_ROW, 0, 0)]
    pallas_call x1, Pallas kernels: 1.86 us -> 3.08 us  [degrees(): pl.pallas_call(degree_kernel, in_specs=[pl.BlockSpec(memory_space=pltpu.S...]
  transfers between devices with their start and end apart: 1 -> 1, of which waited for: 0 -> 1; matrix products, arithmetic and copies ran while one was open for 0% -> 0% of each run, Pallas kernels for 2% -> 1%
where the time goes in v8:
time: 91.1 us; the launch traced here: 90.8 us
  blocking collectives  78.4 us (86%)
  Pallas kernels  8.21 us (9%)
  starting transfers between devices  2.18 us (2%)
  between operations  1.35 us (1%)
    all_to_all x1, blocking collectives, body(): recv_a = lax.all_to_all(send, SAME_CORE_ROW, 0, 0)  28.5 us
    all_to_all x2, blocking collectives, gather(): lax.all_to_all(jnp.broadcast_to(x[None], (count,) + x.shape), axes, 0, 0)  23.6 us
    all_to_all x1, blocking collectives, body(): received = lax.all_to_all(partial, COL, 0, 0)  16.5 us
    all_to_all x1, blocking collectives, body(): own_terms = jnp.sum(lax.all_to_all(terms, NEAR, 0, 0), axis=0)  9.72 us
    pallas_call x1, Pallas kernels, degrees(): pl.pallas_call(degree_kernel, in_specs=[pl.BlockSpec(memory_space=pltpu.S...  3.08 us
    pallas_call x1, Pallas kernels, product(): pl.pallas_call(product_kernel, in_specs=[pl.BlockSpec(memory_space=pltpu....  2.64 us
    ppermute x1, starting transfers between devices, body(): recv_b = lax.ppermute(recv_a, 'core', SWAP)  2.18 us
  transfers between devices with their start and end apart: 1, of which 1 were waited for; matrix products, arithmetic and copies ran while one was open for 0% of the time, Pallas kernels for 1%

profile of v8, /device:TPU:1, one launch (start us, length us, event | category | flops | bytes accessed | tf_op | source)
XLA Modules:
  0.0 90.8 jit_solution(9125892636389495533)
XLA Ops:
  1.3 3.1 %degrees.1 = (bf16[16,160,128]{2,1,0:T(8,128)(2,1)S(1)}, s32[1,256]{1,0:T(1,128)S(4)}, bf16[257,128,128]{2,1,0:T(8,128)(2,1)S(1)}) custom-call(s32[1,1]{1,0:T(1,128)S(6)} %copy.13.count, s32[256]{0:T(256)} %perm_hbm.1, s32[2,256]{1,0:T(2,128)} %bitcast.6, bf16[128,128]{1,0:T(8,128)(2,1)} %feats_hbm.1, bf16[256,128,128]{2,1,0:T(8,128)(2,1)} %bitcast.5), custom_call_target="tpu_custom_call" | custom-call | tf_op jit(solution)/shard_map/degrees/pallas_call | solution.py:105
  4.4 28.5 %all_to_all.25.recv_a = bf16[16,160,128]{2,1,0:T(8,128)(2,1)S(1)} all-to-all(bf16[16,160,128]{2,1,0:T(8,128)(2,1)S(1)} %get-tuple-element.12), channel_id=1, replica_groups=mesh['z'=8,'y_lo'=2,'core'=2,'y_hi'=2,'x'=4] {'z','y_lo'}, dimensions={0} | all-to-all | bytes 1310720 | tf_op jit(solution)/shard_map/all_to_all | solution.py:285
  32.9 2.2 %collective-permute-start = (bf16[16,160,128]{2,1,0:T(8,128)(2,1)S(1)}, bf16[16,160,128]{2,1,0:T(8,128)(2,1)S(1)}, u32[]{:S(2)}, u32[]{:S(2)}) collective-permute-start(bf16[16,160,128]{2,1,0:T(8,128)(2,1)S(1)} %all_to_all.25.recv_a), channel_id=1, source_target_pairs={{0,8},{8,0},{1,9},{9,1},{2,10},{10,2},{3,11},{11,3},{4,12},{12,4},... | collective-permute-start | bytes 1966088 | tf_op jit(solution)/shard_map/ppermute | solution.py:286
  35.1 0.0 copy-start
  35.1 0.0 copy-start.1
  35.1 0.0 copy-start.2
  35.1 1.3 %row_sums.1.sums = bf16[8,16,128]{2,1,0:T(8,128)(2,1)S(1)} custom-call(s32[1,256]{1,0:T(1,128)S(4)} %get-tuple-element.11.slots, bf16[257,128,128]{2,1,0:T(8,128)(2,1)S(1)} %get-tuple-element.13.tiles), custom_call_target="tpu_custom_call" | custom-call | bytes 6291456 | tf_op jit(solution)/shard_map/row_sums/pallas_call | solution.py:154
  36.4 0.4 collective-permute-done.recv_b
  36.8 2.6 %product.1 = bf16[8,144,128]{2,1,0:T(8,128)(2,1)S(1)} custom-call(s32[1,256]{1,0:T(1,128)S(4)} %get-tuple-element.11.slots, bf16[16,160,128]{2,1,0:T(8,128)(2,1)S(1)} %all_to_all.25.recv_a, bf16[16,160,128]{2,1,0:T(8,128)(2,1)S(1)} %collective-permute-done.recv_b, bf16[257,128,128]{2,1,0:T(8,128)(2,1)S(1)} %get-tuple-element.13.tiles, ...), custom_call_target="tpu_custom_call" | custom-call | tf_op jit(solution)/shard_map/product/pallas_call | solution.py:201
  39.4 16.5 %all_to_all.26.parts = bf16[8,144,128]{2,1,0:T(8,128)(2,1)S(1)} all-to-all(bf16[8,144,128]{2,1,0:T(8,128)(2,1)S(1)} %product.1), channel_id=1, replica_groups=mesh['z'=8,'y_lo'=2,'core'=2,'y_hi'=2,'x'=4] {'y_hi','x'}, dimensions={0} | all-to-all | bytes 589824 | tf_op jit(solution)/shard_map/all_to_all | solution.py:288
  55.9 0.0 copy-done
  55.9 0.0 copy-done.1
  55.9 0.0 copy-done.2
  55.9 0.5 nodes.1
  56.4 9.7 %all_to_all.27 = f32[16,17,1,128]{3,2,1,0:T(1,128)S(1)} all-to-all(f32[16,17,1,128]{3,2,1,0:T(1,128)S(1)} %get-tuple-element.14), channel_id=1, replica_groups=mesh['z'=8,'y_lo'=2,'core'=2,'y_hi'=2,'x'=4] {'y_lo','core','x'}, dimensions={0} | all-to-all | bytes 278528 | tf_op jit(solution)/shard_map/all_to_all | solution.py:290
  66.1 0.1 reduce_sum.18
  66.2 0.1 broadcast_in_dim.7
  66.3 13.0 %all_to_all.28 = f32[16,17,1,128]{3,2,1,0:T(1,128)S(1)} all-to-all(f32[16,17,1,128]{3,2,1,0:T(1,128)S(1)} %broadcast_in_dim.7), channel_id=1, replica_groups=mesh['z'=8,'y_lo'=2,'core'=2,'y_hi'=2,'x'=4] {'z','y_hi'}, dimensions={0} | all-to-all | bytes 278528 | tf_op jit(solution)/shard_map/all_to_all | solution.py:275
  79.3 0.1 reduce_sum.19
  79.4 0.1 broadcast_in_dim.8
  79.5 10.7 %all_to_all.29.every = f32[16,17,1,128]{3,2,1,0:T(1,128)S(1)} all-to-all(f32[16,17,1,128]{3,2,1,0:T(1,128)S(1)} %broadcast_in_dim.8), channel_id=1, replica_groups=mesh['z'=8,'y_lo'=2,'core'=2,'y_hi'=2,'x'=4] {'y_lo','core','x'}, dimensions={0} | all-to-all | bytes 278528 | tf_op jit(solution)/shard_map/all_to_all | solution.py:275
  90.1 0.7 finish.1
  (1 shorter events, 0.0 us)
Async XLA Ops:
  32.9 3.9 %collective-permute-start = (bf16[16,160,128]{2,1,0:T(8,128)(2,1)S(1)}, bf16[16,160,128]{2,1,0:T(8,128)(2,1)S(1)}, u32[]{:S(2)}, u32[]{:S(2)}) collective-permute-start(bf16[16,160,128]{2,1,0:T(8,128)(2,1)S(1)} %all_to_all.25.recv_a), channel_id=1, source_target_pairs={{0,8},{8,0},{1,9},{9,1},{2,10},{10,2},{3,11},{11,3},{4,12},{12,4},... | collective-permute-start | bytes 1966088 | tf_op jit(solution)/shard_map/ppermute | solution.py:286
  35.1 20.8 %copy-start = (bf16[128,256]{1,0:T(8,128)(2,1)S(1)}, bf16[128,256]{1,0:T(8,128)(2,1)}, u32[]{:S(2)}) copy-start(bf16[128,256]{1,0:T(8,128)(2,1)} %weight.1) | copy-start | bytes 196612
  35.1 20.8 %copy-start.1 = (bf16[128,256]{1,0:T(8,128)(2,1)S(1)}, bf16[128,256]{1,0:T(8,128)(2,1)}, u32[]{:S(2)}) copy-start(bf16[128,256]{1,0:T(8,128)(2,1)} %cotangent.1) | copy-start | bytes 196612
  35.1 20.9 %copy-start.2 = (f32[256]{0:T(256)S(1)}, f32[256]{0:T(256)}, u32[]{:S(2)}) copy-start(f32[256]{0:T(256)} %param.10) | copy-start | bytes 3076

commit v9 on v8

--- a/solution.py
+++ b/solution.py
@@ -94,8 +94,9 @@
     col_part += jnp.dot(pick, low, preferred_element_type=F32)
     slot_copy.wait()
     feats_copy.wait()
+    turned = feats[...].astype(F32).T.astype(BF16)
     for m in range(16):
-        send_ref[m, 0:128, :] = feats[...]
+        send_ref[m, 0:128, :] = turned
         send_ref[m, 128:160, :] = col_part.astype(BF16)
 
 
@@ -163,16 +164,16 @@
     )(slots, tiles)
 
 
-def product_kernel(slots, recv_a, recv_b, tiles, sums, out, rhs, acc):
+def product_kernel(slots, recv_a, recv_b, tiles, sums, out, lhs, acc):
     from_a = jnp.sum(recv_a[:, 128:160, :].astype(F32), axis=0)
     from_b = jnp.sum(recv_b[:, 128:160, :].astype(F32), axis=0)
     degree = 1.0 + from_a + jnp.concatenate([from_b[16:32], from_b[0:16]], axis=0)
-    scale = jnp.concatenate([lax.rsqrt(degree), jnp.zeros((96, 128), F32)], axis=0).T
+    scale = lax.rsqrt(degree)
     for part in range(4):
         for b in range(part * 8, part * 8 + 8):
             feat = recv_a[b, 0:128, :] if b < 16 else recv_b[b - 16, 0:128, :]
-            scaled = scale[:, b : b + 1] * feat.astype(F32)
-            rhs[b * 128 : b * 128 + 128, :] = scaled.astype(BF16)
+            scaled = scale[b : b + 1, :] * feat.astype(F32)
+            lhs[part, :, b % 8 * 128 : b % 8 * 128 + 128] = scaled.astype(BF16)
         dense = jnp.concatenate(
             [
                 jnp.concatenate(
@@ -182,8 +183,8 @@
             ],
             axis=0,
         )
-        term = jnp.dot(
-            dense, rhs[part * 1024 : part * 1024 + 1024, :], preferred_element_type=F32
+        term = lax.dot_general(
+            lhs[part], dense, (((1,), (1,)), ((), ())), preferred_element_type=F32
         )
         if part == 0:
             acc[...] = term
@@ -192,7 +193,7 @@
         else:
             total = (acc[...] + term).astype(BF16)
     for i in range(8):
-        out[i, 0:128, :] = total[i * 128 : i * 128 + 128, :]
+        out[i, 0:128, :] = total[:, i * 128 : i * 128 + 128]
         out[i, 128:144, :] = sums[i]
 
 
@@ -202,7 +203,7 @@
         product_kernel,
         in_specs=[pl.BlockSpec(memory_space=pltpu.SMEM), vmem, vmem, vmem, vmem],
         out_specs=vmem,
-        scratch_shapes=[pltpu.VMEM((4096, 128), BF16), pltpu.VMEM((1024, 128), F32)],
+        scratch_shapes=[pltpu.VMEM((4, 128, 1024), BF16), pltpu.VMEM((128, 1024), F32)],
         out_shape=jax.ShapeDtypeStruct((8, 144, 128), BF16),
         compiler_params=pltpu.CompilerParams(vmem_limit_bytes=24 << 20),
         name="product",
@@ -211,17 +212,18 @@
 
 def node_kernel(parts, weight, bias, cotangent, hidden_ref, terms_ref):
     total = jnp.sum(parts[...].astype(F32), axis=0)
-    row_degree = jnp.broadcast_to(1.0 + total[128:129, :] + total[136:137, :], (128, 128)).T
+    row_degree = 1.0 + total[128:129, :] + total[136:137, :]
     aggregated = (lax.rsqrt(row_degree) * total[0:128, :]).astype(BF16)
-    preact = jnp.dot(aggregated, weight[...], preferred_element_type=F32) + bias[...]
+    preact = lax.dot_general(
+        aggregated, weight[...], (((0,), (0,)), ((), ())), preferred_element_type=F32
+    )
+    preact += bias[...]
     logistic = jax.nn.sigmoid(preact)
     hidden_ref[...] = (preact * logistic).astype(BF16)
     grad = (
         cotangent[...].astype(F32) * logistic * (1.0 + preact * (1.0 - logistic))
     ).astype(BF16)
-    weight_part = lax.dot_general(
-        aggregated, grad, (((0,), (0,)), ((), ())), preferred_element_type=F32
-    )
+    weight_part = jnp.dot(aggregated, grad, preferred_element_type=F32)
     bias_part = jnp.sum(grad.astype(F32), axis=0, keepdims=True)
     for k in range(16):
         for half in range(2):

time: 91.1 us -> 90.7 us (level)
  Pallas kernels: 8.21 us -> 7.22 us
    all_to_all x1, blocking collectives: 28.5 us -> 30.2 us  [body(): recv_a = lax.all_to_all(send, SAME_CORE_ROW, 0, 0)]
    all_to_all x1, blocking collectives: 16.5 us -> 14.9 us  [body(): received = lax.all_to_all(partial, COL, 0, 0)]
    pallas_call x1, Pallas kernels: 3.08 us -> 1.89 us  [degrees(): pl.pallas_call(degree_kernel, in_specs=[pl.BlockSpec(memory_space=pltpu.S...]
  transfers between devices with their start and end apart: 1 -> 1, of which waited for: 1 -> 1; matrix products, arithmetic and copies ran while one was open for 0% -> 0% of each run, Pallas kernels for 1% -> 2%
where the time goes in v9:
time: 90.7 us; the launch traced here: 89.9 us
  blocking collectives  78.5 us (87%)
  Pallas kernels  7.22 us (8%)
  starting transfers between devices  2.18 us (2%)
  between operations  1.35 us (1%)
    all_to_all x1, blocking collectives, body(): recv_a = lax.all_to_all(send, SAME_CORE_ROW, 0, 0)  30.2 us
    all_to_all x2, blocking collectives, gather(): lax.all_to_all(jnp.broadcast_to(x[None], (count,) + x.shape), axes, 0, 0)  23.6 us
    all_to_all x1, blocking collectives, body(): received = lax.all_to_all(partial, COL, 0, 0)  14.9 us
    all_to_all x1, blocking collectives, body(): own_terms = jnp.sum(lax.all_to_all(terms, NEAR, 0, 0), axis=0)  9.73 us
    pallas_call x1, Pallas kernels, product(): pl.pallas_call(product_kernel, in_specs=[pl.BlockSpec(memory_space=pltpu....  2.85 us
    ppermute x1, starting transfers between devices, body(): recv_b = lax.ppermute(recv_a, 'core', SWAP)  2.18 us
    pallas_call x1, Pallas kernels, degrees(): pl.pallas_call(degree_kernel, in_specs=[pl.BlockSpec(memory_space=pltpu.S...  1.89 us
  transfers between devices with their start and end apart: 1, of which 1 were waited for; matrix products, arithmetic and copies ran while one was open for 0% of the time, Pallas kernels for 2%

profile of v9, /device:TPU:1, one launch (start us, length us, event | category | flops | bytes accessed | tf_op | source)
XLA Modules:
  0.0 89.9 jit_solution(17916073958707721962)
XLA Ops:
  1.3 1.9 %degrees.1 = (bf16[16,160,128]{2,1,0:T(8,128)(2,1)S(1)}, s32[1,256]{1,0:T(1,128)S(4)}, bf16[257,128,128]{2,1,0:T(8,128)(2,1)S(1)}) custom-call(s32[1,1]{1,0:T(1,128)S(6)} %copy.13.count, s32[256]{0:T(256)} %perm_hbm.1, s32[2,256]{1,0:T(2,128)} %bitcast.6, bf16[128,128]{1,0:T(8,128)(2,1)} %feats_hbm.1, bf16[256,128,128]{2,1,0:T(8,128)(2,1)} %bitcast.5), custom_call_target="tpu_custom_call" | custom-call | tf_op jit(solution)/shard_map/degrees/pallas_call | solution.py:106
  3.2 30.2 %all_to_all.25.recv_a = bf16[16,160,128]{2,1,0:T(8,128)(2,1)S(1)} all-to-all(bf16[16,160,128]{2,1,0:T(8,128)(2,1)S(1)} %get-tuple-element.12), channel_id=1, replica_groups=mesh['z'=8,'y_lo'=2,'core'=2,'y_hi'=2,'x'=4] {'z','y_lo'}, dimensions={0} | all-to-all | bytes 1310720 | tf_op jit(solution)/shard_map/all_to_all | solution.py:287
  33.4 2.2 %collective-permute-start = (bf16[16,160,128]{2,1,0:T(8,128)(2,1)S(1)}, bf16[16,160,128]{2,1,0:T(8,128)(2,1)S(1)}, u32[]{:S(2)}, u32[]{:S(2)}) collective-permute-start(bf16[16,160,128]{2,1,0:T(8,128)(2,1)S(1)} %all_to_all.25.recv_a), channel_id=1, source_target_pairs={{0,8},{8,0},{1,9},{9,1},{2,10},{10,2},{3,11},{11,3},{4,12},{12,4},... | collective-permute-start | bytes 1966088 | tf_op jit(solution)/shard_map/ppermute | solution.py:288
  35.5 0.0 copy-start
  35.5 0.0 copy-start.1
  35.5 0.0 copy-start.2
  35.5 1.3 %row_sums.1.sums = bf16[8,16,128]{2,1,0:T(8,128)(2,1)S(1)} custom-call(s32[1,256]{1,0:T(1,128)S(4)} %get-tuple-element.11.slots, bf16[257,128,128]{2,1,0:T(8,128)(2,1)S(1)} %get-tuple-element.13.tiles), custom_call_target="tpu_custom_call" | custom-call | bytes 6291456 | tf_op jit(solution)/shard_map/row_sums/pallas_call | solution.py:155
  36.9 0.4 collective-permute-done.recv_b
  37.3 2.8 %product.1 = bf16[8,144,128]{2,1,0:T(8,128)(2,1)S(1)} custom-call(s32[1,256]{1,0:T(1,128)S(4)} %get-tuple-element.11.slots, bf16[16,160,128]{2,1,0:T(8,128)(2,1)S(1)} %all_to_all.25.recv_a, bf16[16,160,128]{2,1,0:T(8,128)(2,1)S(1)} %collective-permute-done.recv_b, bf16[257,128,128]{2,1,0:T(8,128)(2,1)S(1)} %get-tuple-element.13.tiles, ...), custom_call_target="tpu_custom_call" | custom-call | tf_op jit(solution)/shard_map/product/pallas_call | solution.py:202
  40.1 14.9 %all_to_all.26.parts = bf16[8,144,128]{2,1,0:T(8,128)(2,1)S(1)} all-to-all(bf16[8,144,128]{2,1,0:T(8,128)(2,1)S(1)} %product.1), channel_id=1, replica_groups=mesh['z'=8,'y_lo'=2,'core'=2,'y_hi'=2,'x'=4] {'y_hi','x'}, dimensions={0} | all-to-all | bytes 589824 | tf_op jit(solution)/shard_map/all_to_all | solution.py:290
  55.0 0.0 copy-done
  55.1 0.0 copy-done.1
  55.1 0.0 copy-done.2
  55.1 0.4 nodes.1
  55.5 9.7 %all_to_all.27 = f32[16,17,1,128]{3,2,1,0:T(1,128)S(1)} all-to-all(f32[16,17,1,128]{3,2,1,0:T(1,128)S(1)} %get-tuple-element.14), channel_id=1, replica_groups=mesh['z'=8,'y_lo'=2,'core'=2,'y_hi'=2,'x'=4] {'y_lo','core','x'}, dimensions={0} | all-to-all | bytes 278528 | tf_op jit(solution)/shard_map/all_to_all | solution.py:292
  65.2 0.1 reduce_sum.18
  65.3 0.1 broadcast_in_dim.7
  65.4 13.0 %all_to_all.28 = f32[16,17,1,128]{3,2,1,0:T(1,128)S(1)} all-to-all(f32[16,17,1,128]{3,2,1,0:T(1,128)S(1)} %broadcast_in_dim.7), channel_id=1, replica_groups=mesh['z'=8,'y_lo'=2,'core'=2,'y_hi'=2,'x'=4] {'z','y_hi'}, dimensions={0} | all-to-all | bytes 278528 | tf_op jit(solution)/shard_map/all_to_all | solution.py:277
  78.4 0.1 reduce_sum.19
  78.5 0.1 broadcast_in_dim.8
  78.6 10.7 %all_to_all.29.every = f32[16,17,1,128]{3,2,1,0:T(1,128)S(1)} all-to-all(f32[16,17,1,128]{3,2,1,0:T(1,128)S(1)} %broadcast_in_dim.8), channel_id=1, replica_groups=mesh['z'=8,'y_lo'=2,'core'=2,'y_hi'=2,'x'=4] {'y_lo','core','x'}, dimensions={0} | all-to-all | bytes 278528 | tf_op jit(solution)/shard_map/all_to_all | solution.py:277
  89.3 0.7 finish.1
  (1 shorter events, 0.0 us)
Async XLA Ops:
  33.4 3.9 %collective-permute-start = (bf16[16,160,128]{2,1,0:T(8,128)(2,1)S(1)}, bf16[16,160,128]{2,1,0:T(8,128)(2,1)S(1)}, u32[]{:S(2)}, u32[]{:S(2)}) collective-permute-start(bf16[16,160,128]{2,1,0:T(8,128)(2,1)S(1)} %all_to_all.25.recv_a), channel_id=1, source_target_pairs={{0,8},{8,0},{1,9},{9,1},{2,10},{10,2},{3,11},{11,3},{4,12},{12,4},... | collective-permute-start | bytes 1966088 | tf_op jit(solution)/shard_map/ppermute | solution.py:288
  35.5 19.5 %copy-start = (bf16[128,256]{1,0:T(8,128)(2,1)S(1)}, bf16[128,256]{1,0:T(8,128)(2,1)}, u32[]{:S(2)}) copy-start(bf16[128,256]{1,0:T(8,128)(2,1)} %weight.1) | copy-start | bytes 196612
  35.5 19.5 %copy-start.1 = (bf16[128,256]{1,0:T(8,128)(2,1)S(1)}, bf16[128,256]{1,0:T(8,128)(2,1)}, u32[]{:S(2)}) copy-start(bf16[128,256]{1,0:T(8,128)(2,1)} %cotangent.1) | copy-start | bytes 196612
  35.5 19.5 %copy-start.2 = (f32[256]{0:T(256)S(1)}, f32[256]{0:T(256)}, u32[]{:S(2)}) copy-start(f32[256]{0:T(256)} %param.10) | copy-start | bytes 3076
